TPU v7x, 256 devices: a whole 4x4x8 slice. The times are simulated.
256 devices in a mesh: brick: 128 (over x, z, y), state: 2 (over core).
Axes of the slice: x: 4, y: 4, z: 8, core: 2. Of those that a mesh axis runs over, the one named last changes fastest.
Arguments:
- states: bfloat16 [384, 884736], P('state', 'brick'), may hold values from -40 to 40
- kinetic: bfloat16 [343, 343], replicated, may hold values from -2 to 4, as said below
- potential: float32 [884736], P('brick'), may hold values from -1.5 to 1.5
- cell_nodes: int32 [4096, 343], P('brick'), may hold values from 0 to 8063, as said below
- face_map: int32 [147456], P('brick'), may hold values from 0 to 6911, as said below
Outputs:
- rotated: float32 [384, 884736], P('state', 'brick')
Inputs may be any that keep to these rules, and one draw needn't show every extreme that they name: `cell_nodes`: block b of 32 rows belongs to brick b; a row lists the 343 nodes of one hexahedral cell of degree 6, lexicographic in the cell's three local coordinates, the first slowest. A value below 6912 is a column of brick b's block of states and potential; a value 6912 + f is the node named by entry f of brick b + 1's block of face_map (brick 0 after the last). Every own node and every face slot lies in some cell. `face_map`: block b of 1152 entries lists distinct own nodes of brick b: those it shares with brick b - 1. `kinetic`: Symmetric.
All inputs are finite; a program needn't handle non-finite values.
Results may differ from a plain program's by a relative error of at most 0.0005.
The roundings to bfloat16 on the way count: a program that leaves them out, or rounds other values in their place, can miss the bound.
Values may be sent and summed in bfloat16 or wider, within the bound.
A program may use at most 128 MiB of HBM per device.

v0:
```python
import jax
import jax.numpy as jnp
from jax import lax
from jax.sharding import PartitionSpec as P

NS_STEPS = 3


cheb_center = 3.0
cheb_half = 7.0
epsilon = 1e-06


def passed_along(value, axis, steps):
    count = lax.axis_size(axis)
    pairs = [(source, (source + steps) % count) for source in range(count)]
    return lax.ppermute(value, axis, pairs)


def apply_operator(vector, kinetic, potential, cell_nodes, face_map):
    width, owned = vector.shape
    face_count = face_map.shape[0]
    ghost_cols = passed_along(vector[:, face_map], "brick", -1)
    extended = jnp.concatenate([vector, ghost_cols], axis=1)
    gathered = extended[:, cell_nodes]
    products = jnp.einsum("wca,ea->wce", gathered, kinetic, preferred_element_type=jnp.float32)
    summed = (
        jnp.zeros((width, owned + face_count), jnp.float32)
        .at[:, cell_nodes.reshape(-1)]
        .add(products.reshape(width, -1))
    )
    returned = passed_along(summed[:, owned:], "brick", 1)
    assembled = summed[:, :owned].at[:, face_map].add(returned)
    return assembled + potential[None, :] * vector.astype(jnp.float32)


def row_newton_schulz(margin_rows, start):
    height, total = margin_rows.shape
    square_part = jnp.sum(margin_rows * margin_rows)
    scale = jnp.sqrt(lax.psum(square_part, "state") + epsilon)
    current_rows = margin_rows / scale
    row_ids = lax.broadcasted_iota(jnp.int32, (height, total), 0) + start
    column_ids = lax.broadcasted_iota(jnp.int32, (height, total), 1)
    inverse_rows = (row_ids == column_ids).astype(jnp.float32)
    three_rows = 3.0 * inverse_rows
    for iteration in range(NS_STEPS):
        current_full, inverse_full = (
            lax.all_gather(current_rows, "state", axis=0, tiled=True),
            lax.all_gather(inverse_rows, "state", axis=0, tiled=True),
        )
        factor_rows = three_rows - jnp.dot(
            inverse_rows, current_full, precision=lax.Precision.HIGHEST
        )
        current_rows = 0.5 * jnp.dot(factor_rows, current_full, precision=lax.Precision.HIGHEST)
        inverse_rows = 0.5 * jnp.dot(factor_rows, inverse_full, precision=lax.Precision.HIGHEST)
    return inverse_rows


def local(states, kinetic, potential, cell_nodes, face_map):
    first = apply_operator(states, kinetic, potential, cell_nodes, face_map)
    filtered_once = ((first - cheb_center * states.astype(jnp.float32)) / cheb_half).astype(
        jnp.bfloat16
    )
    second = apply_operator(filtered_once, kinetic, potential, cell_nodes, face_map)
    filtered = (
        2.0 * (second - cheb_center * filtered_once.astype(jnp.float32)) / cheb_half
        - states.astype(jnp.float32)
    ).astype(jnp.bfloat16)
    width = states.shape[0]
    every = lax.all_gather(filtered, "state", axis=0, tiled=True)
    start = lax.axis_index("state") * width
    partial_rows = lax.dot_general(
        filtered, every, (((1,), (1,)), ((), ())), preferred_element_type=jnp.float32
    )
    margin_rows = lax.psum(partial_rows, "brick")
    root_rows = row_newton_schulz(margin_rows, start)
    return jnp.dot(root_rows.astype(jnp.bfloat16), every, preferred_element_type=jnp.float32)


def solution(mesh):
    in_specs = (P("state", "brick"), P(), P("brick"), P("brick", None), P("brick"))
    out_specs = P("state", "brick")
    return jax.shard_map(local, mesh=mesh, in_specs=in_specs, out_specs=out_specs, check_vma=False)
```

profile of v0, /device:TPU:1, one launch (start us, length us, event | category | flops | bytes accessed | tf_op | source)
XLA Modules:
  0.0 724.0 jit_solution(10904501136312395862)
XLA Ops:
  12.8 5.7 gather_fusion
  18.8 11.4 %collective-permute-start = (bf16[192,1152]{1,0:T(8,128)(2,1)S(1)}, bf16[192,1152]{1,0:T(8,128)(2,1)S(1)}, u32[]{:S(2)}, u32[]{:S(2)}) collective-permute-start(bf16[192,1152]{1,0:T(8,128)(2,1)S(1)} %copy.37), channel_id=1, source_target_pairs={{0,254},{2,0},{4,2},{6,4},{8,6},{10,8},{12,10},{14,12},{16,14},{18... | collective-permute-start | bytes 1327112 | tf_op jit(solution)/shard_map/ppermute | solution.py:17
  30.7 8.4 %collective-permute-done = bf16[192,1152]{1,0:T(8,128)(2,1)S(1)} collective-permute-done((bf16[192,1152]{1,0:T(8,128)(2,1)S(1)}, bf16[192,1152]{1,0:T(8,128)(2,1)S(1)}, u32[]{:S(2)}, u32[]{:S(2)}) %collective-permute-start) | collective-permute-done | bytes 442400 | tf_op jit(solution)/shard_map/ppermute | solution.py:17
  44.0 28.3 %gather_fusion.1 = bf16[10976,192]{1,0:T(8,128)(2,1)} fusion(bf16[192,8064]{0,1:T(8,128)(2,1)} %pad_maximum_fusion, s32[11264]{0:T(1024)S(1)} %pad_clamp_fusion), kind=kCustom, calls=%fused_computation.1 | custom fusion | bytes 8473472 | tf_op jit(solution)/shard_map/gather | solution.py:25
  72.3 7.5 %copy.40 = bf16[10976,192]{0,1:T(8,128)(2,1)} copy(bf16[10976,192]{1,0:T(8,128)(2,1)} %gather_fusion.1) | data formatting | bytes 8429568 | tf_op jit(solution)/shard_map/gather | solution.py:25
  79.8 12.8 %reshape.55 = bf16[32,343,192]{1,0,2:T(8,128)(2,1)} reshape(bf16[10976,192]{0,1:T(8,128)(2,1)} %copy.40) | data formatting | bytes 8429568 | tf_op jit(solution)/shard_map/gather | solution.py:25
  92.6 9.0 %fusion.10 = f32[192,32,343]{2,1,0:T(8,128)} fusion(bf16[32,343,192]{1,0,2:T(8,128)(2,1)} %reshape.55, bf16[343,343]{1,0:T(8,128)(2,1)S(1)} %copy-done), kind=kOutput, calls=%fused_computation.23 | convolution fusion | flops 1445670912 | bytes 12879650 | tf_op jit(solution)/shard_map/wca,ea->wce/dot_general | solution.py:26
  101.6 11.1 %reshape.75 = f32[192,10976]{1,0:T(8,128)} reshape(f32[192,32,343]{2,1,0:T(8,128)} %fusion.10) | data formatting | bytes 16859136 | tf_op jit(solution)/shard_map/reshape | solution.py:30
  112.7 10.6 %copy.43 = f32[10976,192]{1,0:T(8,128)} copy(f32[10976,192]{0,1:T(8,128)} %bitcast.40) | data formatting | bytes 16859136 | tf_op jit(solution)/shard_map/reshape | solution.py:30
  123.3 59.6 %scatter_custom_fusion = f32[192,8064]{0,1:T(8,128)} fusion(s32[10976]{0:T(1024)S(1)} %fusion.21, f32[10976,192]{1,0:T(8,128)} %copy.43, f32[]{:T(128)} %constant.14.clone.1), kind=kCustom, calls=%fused_computation.29 | custom fusion | flops 2107392 | bytes 6193664 | tf_op jit(solution)/shard_map/scatter-add | solution.py:30
  184.7 7.3 %fusion.3 = f32[192,6912]{0,1:T(8,128)} fusion(bf16[192,6912]{0,1:T(8,128)(2,1)} %copy.38, f32[192,8064]{0,1:T(8,128)} %scatter_custom_fusion, f32[6912]{0:T(1024)S(1)} %copy-done.2), kind=kLoop, calls=%fused_computation.16 | loop fusion | flops 3981312 | bytes 13298688 | tf_op jit(solution)/shard_map/add.1
  192.0 18.8 %collective-permute-done.1 = f32[192,1152]{1,0:T(8,128)S(1)} collective-permute-done((f32[192,1152]{1,0:T(8,128)S(1)}, f32[192,1152]{1,0:T(8,128)S(1)}, u32[]{:S(2)}, u32[]{:S(2)}) %collective-permute-start.1) | collective-permute-done | bytes 884768 | tf_op jit(solution)/shard_map/ppermute | solution.py:17
  211.2 14.7 %scatter_fusion = f32[192,6912]{0,1:T(8,128)} fusion(f32[192,6912]{0,1:T(8,128)} %fusion.3, s32[1152]{0:T(1024)S(1)} %compare_select_fusion.2, f32[1152,192]{1,0:T(8,128)S(1)} %copy.46), kind=kCustom, calls=%fused_computation.5 | custom fusion | flops 221184 | bytes 2658816 | tf_op jit(solution)/shard_map/scatter-add | solution.py:33
  225.9 7.0 fusion.6
  232.9 5.7 gather_fusion.2
  240.3 8.4 %collective-permute-done.2 = bf16[192,1152]{1,0:T(8,128)(2,1)S(1)} collective-permute-done((bf16[192,1152]{1,0:T(8,128)(2,1)S(1)}, bf16[192,1152]{1,0:T(8,128)(2,1)S(1)}, u32[]{:S(2)}, u32[]{:S(2)}) %collective-permute-start.2) | collective-permute-done | bytes 442400 | tf_op jit(solution)/shard_map/ppermute | solution.py:17
  253.7 28.3 %gather_fusion.3 = bf16[10976,192]{1,0:T(8,128)(2,1)} fusion(bf16[192,8064]{0,1:T(8,128)(2,1)} %pad_maximum_fusion.1, s32[11264]{0:T(1024)S(1)} %pad_clamp_fusion), kind=kCustom, calls=%fused_computation.3 | custom fusion | bytes 8473472 | tf_op jit(solution)/shard_map/gather | solution.py:25
  282.0 7.5 %copy.49 = bf16[10976,192]{0,1:T(8,128)(2,1)} copy(bf16[10976,192]{1,0:T(8,128)(2,1)} %gather_fusion.3) | data formatting | bytes 8429568 | tf_op jit(solution)/shard_map/gather | solution.py:25
  289.5 12.8 %reshape.71 = bf16[32,343,192]{1,0,2:T(8,128)(2,1)} reshape(bf16[10976,192]{0,1:T(8,128)(2,1)} %copy.49) | data formatting | bytes 8429568 | tf_op jit(solution)/shard_map/gather | solution.py:25
  302.3 9.0 %fusion.8 = f32[192,32,343]{2,1,0:T(8,128)} fusion(bf16[32,343,192]{1,0,2:T(8,128)(2,1)} %reshape.71, bf16[343,343]{1,0:T(8,128)(2,1)S(1)} %copy-done), kind=kOutput, calls=%fused_computation.21 | convolution fusion | flops 1445670912 | bytes 12879650 | tf_op jit(solution)/shard_map/wca,ea->wce/dot_general | solution.py:26
  311.3 11.1 %reshape.91 = f32[192,10976]{1,0:T(8,128)} reshape(f32[192,32,343]{2,1,0:T(8,128)} %fusion.8) | data formatting | bytes 16859136 | tf_op jit(solution)/shard_map/reshape | solution.py:30
  322.3 10.6 %copy.52 = f32[10976,192]{1,0:T(8,128)} copy(f32[10976,192]{0,1:T(8,128)} %bitcast.41) | data formatting | bytes 16859136 | tf_op jit(solution)/shard_map/reshape | solution.py:30
  332.9 59.1 %scatter_custom_fusion.2 = f32[192,8064]{0,1:T(8,128)} fusion(s32[10976]{0:T(1024)S(1)} %fusion.21, f32[10976,192]{1,0:T(8,128)} %copy.52, f32[]{:T(128)} %constant.14.clone.1), kind=kCustom, calls=%fused_computation.27 | custom fusion | flops 2107392 | bytes 6193664 | tf_op jit(solution)/shard_map/scatter-add | solution.py:30
  394.1 7.3 %fusion = f32[192,6912]{0,1:T(8,128)} fusion(bf16[192,6912]{0,1:T(8,128)(2,1)} %fusion.6, f32[192,8064]{0,1:T(8,128)} %scatter_custom_fusion.2, f32[6912]{0:T(1024)S(1)} %copy-done.2), kind=kLoop, calls=%fused_computation.13 | loop fusion | flops 3981312 | bytes 13298688 | tf_op jit(solution)/shard_map/add.2
  401.4 16.3 %collective-permute-done.3 = f32[192,1152]{1,0:T(8,128)S(1)} collective-permute-done((f32[192,1152]{1,0:T(8,128)S(1)}, f32[192,1152]{1,0:T(8,128)S(1)}, u32[]{:S(2)}, u32[]{:S(2)}) %collective-permute-start.3) | collective-permute-done | bytes 884768 | tf_op jit(solution)/shard_map/ppermute | solution.py:17
  418.1 14.7 %scatter_fusion.1 = f32[192,6912]{0,1:T(8,128)} fusion(f32[192,6912]{0,1:T(8,128)} %fusion, s32[1152]{0:T(1024)S(1)} %compare_select_fusion.2, f32[1152,192]{1,0:T(8,128)S(1)} %copy.54), kind=kCustom, calls=%fused_computation.7 | custom fusion | flops 221184 | bytes 2658816 | tf_op jit(solution)/shard_map/scatter-add | solution.py:33
  432.8 8.4 %fusion.7 = bf16[192,6912]{0,1:T(8,128)(2,1)} fusion(bf16[192,6912]{0,1:T(8,128)(2,1)} %copy.38, f32[192,6912]{0,1:T(8,128)} %scatter_fusion.1, bf16[192,6912]{0,1:T(8,128)(2,1)} %fusion.6), kind=kLoop, calls=%fused_computation.20 | loop fusion | flops 9289728 | bytes 13271040 | tf_op jit(solution)/shard_map/convert_element_type | solution.py:68
  441.2 5.6 copy.55
  446.9 16.5 %all-gather.2.cloned.1.call-done = bf16[384,6912]{1,0:T(8,128)(2,1)} async-done(((bf16[192,6912]{1,0:T(8,128)(2,1)}), bf16[384,6912]{1,0:T(8,128)(2,1)}) %all-gather.2.cloned.1.call-update) | async-done | bytes 5308432 | tf_op jit(solution)/shard_map/all_gather | solution.py:70
  463.4 6.5 fusion.22
  470.0 212.0 %all-reduce.2.cloned.1.call-done = f32[192,384]{1,0:T(8,128)} async-done(((f32[192,384]{1,0:T(8,128)}), f32[192,384]{1,0:T(8,128)}) %all-reduce.2.cloned.1.call-update) | async-done | bytes 294928 | tf_op jit(solution)/shard_map/psum | solution.py:75
  683.8 7.0 all_gather.23
  (57 shorter events, 50.3 us)
Async XLA Ops:
  6.5 86.1 %copy-start = (bf16[343,343]{1,0:T(8,128)(2,1)S(1)}, bf16[343,343]{1,0:T(8,128)(2,1)}, u32[]{:S(2)}) copy-start(bf16[343,343]{1,0:T(8,128)(2,1)} %param.6) | copy-start | bytes 705898
  6.5 23.7 %copy-start.1 = (s32[32,343]{1,0:T(8,128)S(1)}, s32[32,343]{1,0:T(8,128)}, u32[]{:S(2)}) copy-start(s32[32,343]{1,0:T(8,128)} %param.8) | copy-start | bytes 131716
  6.5 456.8 %all-gather.2.cloned.1.call-start = ((), (), s32[]{:S(2)}) async-start(), calls=%async_computation | async-start | bytes 7962624 | tf_op jit(solution)/shard_map/all_gather | solution.py:70
  18.8 20.3 %collective-permute-start = (bf16[192,1152]{1,0:T(8,128)(2,1)S(1)}, bf16[192,1152]{1,0:T(8,128)(2,1)S(1)}, u32[]{:S(2)}, u32[]{:S(2)}) collective-permute-start(bf16[192,1152]{1,0:T(8,128)(2,1)S(1)} %copy.37), channel_id=1, source_target_pairs={{0,254},{2,0},{4,2},{6,4},{8,6},{10,8},{12,10},{14,12},{16,14},{18... | collective-permute-start | bytes 1327112 | tf_op jit(solution)/shard_map/ppermute | solution.py:17
  123.3 61.4 %copy-start.2 = (f32[6912]{0:T(1024)S(1)}, f32[6912]{0:T(1024)}, u32[]{:S(2)}) copy-start(f32[6912]{0:T(1024)} %param.7) | copy-start | bytes 82948
  184.6 26.2 %collective-permute-start.1 = (f32[192,1152]{1,0:T(8,128)S(1)}, f32[192,1152]{1,0:T(8,128)S(1)}, u32[]{:S(2)}, u32[]{:S(2)}) collective-permute-start(f32[192,1152]{1,0:T(8,128)S(1)} %copy.45), channel_id=1, source_target_pairs={{0,2},{2,4},{4,6},{6,8},{8,10},{10,12},{12,14},{14,16},{16,18},{18... | collective-permute-start | bytes 2654216 | tf_op jit(solution)/shard_map/ppermute | solution.py:17
  238.9 9.9 %collective-permute-start.2 = (bf16[192,1152]{1,0:T(8,128)(2,1)S(1)}, bf16[192,1152]{1,0:T(8,128)(2,1)S(1)}, u32[]{:S(2)}, u32[]{:S(2)}) collective-permute-start(bf16[192,1152]{1,0:T(8,128)(2,1)S(1)} %copy.47), channel_id=1, source_target_pairs={{0,254},{2,0},{4,2},{6,4},{8,6},{10,8},{12,10},{14,12},{16,14},{18... | collective-permute-start | bytes 1327112 | tf_op jit(solution)/shard_map/ppermute | solution.py:17
  393.8 24.0 %collective-permute-start.3 = (f32[192,1152]{1,0:T(8,128)S(1)}, f32[192,1152]{1,0:T(8,128)S(1)}, u32[]{:S(2)}, u32[]{:S(2)}) collective-permute-start(f32[192,1152]{1,0:T(8,128)S(1)} %copy.53), channel_id=1, source_target_pairs={{0,2},{2,4},{4,6},{6,8},{8,10},{10,12},{12,14},{14,16},{16,18},{18... | collective-permute-start | bytes 2654216 | tf_op jit(solution)/shard_map/ppermute | solution.py:17
  446.8 235.2 %all-reduce.2.cloned.1.call-start = ((), (), s32[]{:S(2)}) async-start(), calls=%async_computation.1 | async-start | bytes 589824 | tf_op jit(solution)/shard_map/psum | solution.py:75
  682.0 30.9 %slice-start = ((s8[5308416]{0:T(1024)(128)(4,1)}), s8[1114112]{0:T(1024)(128)(4,1)S(1)}, s32[]{:S(2)}) async-start(s8[5308416]{0:T(1024)(128)(4,1)} %bitcast.42), calls=%async_computation.2 | async-start | bytes 2228224
  702.0 10.9 %slice-start.1 = ((s8[5308416]{0:T(1024)(128)(4,1)}), s8[4194304]{0:T(1024)(128)(4,1)S(1)}, s32[]{:S(2)}) async-start(s8[5308416]{0:T(1024)(128)(4,1)} %bitcast.42), calls=%async_computation.3 | async-start | bytes 8388608
Sparse Core Ops, SparseCore 0:
  447.0 16.3 all-gather.1
  470.0 211.9 all-reduce.1
where the time goes:
time: 729 us; the launch traced here: 724 us
  waiting for transfers between devices  280 us (38%)
  other arithmetic  191 us (26%)
  local copies, waits for them, and re-layouts  169 us (23%)
  matrix products  34.2 us (5%)
  blocking collectives  21.6 us (3%)
  between operations  14.6 us (2%)
  starting transfers between devices  13.3 us (2%)
    psum x1, waiting for transfers between devices, local(): margin_rows = lax.psum(partial_rows, 'brick')  212 us
    scatter-add x2, other arithmetic, apply_operator(): summed = jnp.zeros((width, owned + face_count), jnp.float32).at[:, cell_n...  119 us
    gather x6, local copies, waits for them, and re-layouts, apply_operator(): gathered = extended[:, cell_nodes]  97.3 us
    ppermute x4, waiting for transfers between devices, passed_along(): return lax.ppermute(value, axis, pairs)  51.9 us
    reshape x4, local copies, waits for them, and re-layouts, apply_operator(): products.reshape(width, -1)  43.3 us
    scatter-add x2, other arithmetic, apply_operator(): assembled = summed[:, :owned].at[:, face_map].add(returned)  29.5 us
    dot_general x2, matrix products, apply_operator(): jnp.einsum('wca,ea->wce', gathered, kinetic, preferred_element_type=jnp.f...  17.9 us
    all_gather x1, waiting for transfers between devices, local(): every = lax.all_gather(filtered, 'state', axis=0, tiled=True)  16.5 us
  transfers between devices with their start and end apart: 6, of which 6 were waited for; matrix products, arithmetic and copies ran while one was open for 2% of the time, Pallas kernels for 0%

commit v1 on v0

--- a/solution.py
+++ b/solution.py
@@ -34,26 +34,22 @@
     return assembled + potential[None, :] * vector.astype(jnp.float32)
 
 
-def row_newton_schulz(margin_rows, start):
-    height, total = margin_rows.shape
-    square_part = jnp.sum(margin_rows * margin_rows)
-    scale = jnp.sqrt(lax.psum(square_part, "state") + epsilon)
-    current_rows = margin_rows / scale
-    row_ids = lax.broadcasted_iota(jnp.int32, (height, total), 0) + start
-    column_ids = lax.broadcasted_iota(jnp.int32, (height, total), 1)
-    inverse_rows = (row_ids == column_ids).astype(jnp.float32)
-    three_rows = 3.0 * inverse_rows
-    for iteration in range(NS_STEPS):
-        current_full, inverse_full = (
-            lax.all_gather(current_rows, "state", axis=0, tiled=True),
-            lax.all_gather(inverse_rows, "state", axis=0, tiled=True),
-        )
-        factor_rows = three_rows - jnp.dot(
-            inverse_rows, current_full, precision=lax.Precision.HIGHEST
-        )
-        current_rows = 0.5 * jnp.dot(factor_rows, current_full, precision=lax.Precision.HIGHEST)
-        inverse_rows = 0.5 * jnp.dot(factor_rows, inverse_full, precision=lax.Precision.HIGHEST)
-    return inverse_rows
+def newton_schulz(margin):
+    total = margin.shape[0]
+    scale = jnp.sqrt(jnp.sum(margin * margin) + epsilon)
+    current = margin / scale
+    row_ids = lax.broadcasted_iota(jnp.int32, (total, total), 0)
+    column_ids = lax.broadcasted_iota(jnp.int32, (total, total), 1)
+    three = 3.0 * (row_ids == column_ids).astype(jnp.float32)
+    factor = three - current
+    current = 0.5 * jnp.dot(factor, current, precision=lax.Precision.HIGHEST)
+    inverse = 0.5 * factor
+    for iteration in range(1, NS_STEPS):
+        factor = three - jnp.dot(inverse, current, precision=lax.Precision.HIGHEST)
+        if iteration < NS_STEPS - 1:
+            current = 0.5 * jnp.dot(factor, current, precision=lax.Precision.HIGHEST)
+        inverse = 0.5 * jnp.dot(factor, inverse, precision=lax.Precision.HIGHEST)
+    return inverse
 
 
 def local(states, kinetic, potential, cell_nodes, face_map):
@@ -68,12 +64,15 @@
     ).astype(jnp.bfloat16)
     width = states.shape[0]
     every = lax.all_gather(filtered, "state", axis=0, tiled=True)
-    start = lax.axis_index("state") * width
-    partial_rows = lax.dot_general(
-        filtered, every, (((1,), (1,)), ((), ())), preferred_element_type=jnp.float32
+    side = lax.axis_index("state")
+    half = every.shape[1] // 2
+    share = lax.dynamic_slice_in_dim(every, side * half, half, axis=1)
+    partial = lax.dot_general(
+        share, share, (((1,), (1,)), ((), ())), preferred_element_type=jnp.float32
     )
-    margin_rows = lax.psum(partial_rows, "brick")
-    root_rows = row_newton_schulz(margin_rows, start)
+    margin = lax.psum(partial, ("brick", "state"))
+    root = newton_schulz(margin)
+    root_rows = lax.dynamic_slice_in_dim(root, side * width, width, axis=0)
     return jnp.dot(root_rows.astype(jnp.bfloat16), every, preferred_element_type=jnp.float32)
 
 

time: 729 us -> 751 us (1.030)
  waiting for transfers between devices: 280 us -> 322 us
  blocking collectives: 21.6 us -> 0 us
    psum x1, waiting for transfers between devices: 212 us -> 254 us  [local(): margin = lax.psum(partial, ('brick', 'state'))]
    all_gather x6 -> x0, blocking collectives: 18.5 us -> none  [the longest x3 11.8 us: row_newton_schulz(): lax.all_gather(inverse_rows, 'state', axis=0, tiled=True)]
    dot_general x9 -> x7, matrix products: 12.3 us -> 15.2 us  [the longest x1 4.92 us: local(): lax.dot_general(share, share, (((1,), (1,)), ((), ())), preferred_element...]
where the time goes in v1:
time: 751 us; the launch traced here: 746 us
  waiting for transfers between devices  322 us (43%)
  other arithmetic  190 us (25%)
  local copies, waits for them, and re-layouts  169 us (23%)
  matrix products  37 us (5%)
  between operations  14.6 us (2%)
  starting transfers between devices  13.5 us (2%)
    psum x1, waiting for transfers between devices, local(): margin = lax.psum(partial, ('brick', 'state'))  254 us
    scatter-add x2, other arithmetic, apply_operator(): summed = jnp.zeros((width, owned + face_count), jnp.float32).at[:, cell_n...  119 us
    gather x6, local copies, waits for them, and re-layouts, apply_operator(): gathered = extended[:, cell_nodes]  97.3 us
    ppermute x4, waiting for transfers between devices, passed_along(): return lax.ppermute(value, axis, pairs)  51.9 us
    reshape x4, local copies, waits for them, and re-layouts, apply_operator(): products.reshape(width, -1)  43.3 us
    scatter-add x2, other arithmetic, apply_operator(): assembled = summed[:, :owned].at[:, face_map].add(returned)  29.5 us
    dot_general x2, matrix products, apply_operator(): jnp.einsum('wca,ea->wce', gathered, kinetic, preferred_element_type=jnp.f...  17.9 us
    all_gather x1, waiting for transfers between devices, local(): every = lax.all_gather(filtered, 'state', axis=0, tiled=True)  16.2 us
  transfers between devices with their start and end apart: 6, of which 6 were waited for; matrix products, arithmetic and copies ran while one was open for 2% of the time, Pallas kernels for 0%

profile of v1, /device:TPU:1, one launch (start us, length us, event | category | flops | bytes accessed | tf_op | source)
XLA Modules:
  0.0 746.4 jit_solution(6164590468286375535)
XLA Ops:
  6.5 5.6 copy.38
  12.8 5.7 gather_fusion
  18.8 11.4 %collective-permute-start = (bf16[192,1152]{1,0:T(8,128)(2,1)S(1)}, bf16[192,1152]{1,0:T(8,128)(2,1)S(1)}, u32[]{:S(2)}, u32[]{:S(2)}) collective-permute-start(bf16[192,1152]{1,0:T(8,128)(2,1)S(1)} %copy.37), channel_id=1, source_target_pairs={{0,254},{2,0},{4,2},{6,4},{8,6},{10,8},{12,10},{14,12},{16,14},{18... | collective-permute-start | bytes 1327112 | tf_op jit(solution)/shard_map/ppermute | solution.py:17
  30.7 8.4 %collective-permute-done = bf16[192,1152]{1,0:T(8,128)(2,1)S(1)} collective-permute-done((bf16[192,1152]{1,0:T(8,128)(2,1)S(1)}, bf16[192,1152]{1,0:T(8,128)(2,1)S(1)}, u32[]{:S(2)}, u32[]{:S(2)}) %collective-permute-start) | collective-permute-done | bytes 442400 | tf_op jit(solution)/shard_map/ppermute | solution.py:17
  44.0 28.3 %gather_fusion.1 = bf16[10976,192]{1,0:T(8,128)(2,1)} fusion(bf16[192,8064]{0,1:T(8,128)(2,1)} %pad_maximum_fusion, s32[11264]{0:T(1024)S(1)} %pad_clamp_fusion), kind=kCustom, calls=%fused_computation.1 | custom fusion | bytes 8473472 | tf_op jit(solution)/shard_map/gather | solution.py:25
  72.3 7.5 %copy.40 = bf16[10976,192]{0,1:T(8,128)(2,1)} copy(bf16[10976,192]{1,0:T(8,128)(2,1)} %gather_fusion.1) | data formatting | bytes 8429568 | tf_op jit(solution)/shard_map/gather | solution.py:25
  79.8 12.8 %reshape.55 = bf16[32,343,192]{1,0,2:T(8,128)(2,1)} reshape(bf16[10976,192]{0,1:T(8,128)(2,1)} %copy.40) | data formatting | bytes 8429568 | tf_op jit(solution)/shard_map/gather | solution.py:25
  92.6 9.0 %fusion.10 = f32[192,32,343]{2,1,0:T(8,128)} fusion(bf16[32,343,192]{1,0,2:T(8,128)(2,1)} %reshape.55, bf16[343,343]{1,0:T(8,128)(2,1)S(1)} %copy-done), kind=kOutput, calls=%fused_computation.23 | convolution fusion | flops 1445670912 | bytes 12879650 | tf_op jit(solution)/shard_map/wca,ea->wce/dot_general | solution.py:26
  101.6 11.1 %reshape.75 = f32[192,10976]{1,0:T(8,128)} reshape(f32[192,32,343]{2,1,0:T(8,128)} %fusion.10) | data formatting | bytes 16859136 | tf_op jit(solution)/shard_map/reshape | solution.py:30
  112.7 10.6 %copy.43 = f32[10976,192]{1,0:T(8,128)} copy(f32[10976,192]{0,1:T(8,128)} %bitcast.30) | data formatting | bytes 16859136 | tf_op jit(solution)/shard_map/reshape | solution.py:30
  123.3 59.6 %scatter_custom_fusion = f32[192,8064]{0,1:T(8,128)} fusion(s32[10976]{0:T(1024)S(1)} %fusion.35, f32[10976,192]{1,0:T(8,128)} %copy.43, f32[]{:T(128)} %constant.14.clone.1), kind=kCustom, calls=%fused_computation.29 | custom fusion | flops 2107392 | bytes 6193664 | tf_op jit(solution)/shard_map/scatter-add | solution.py:30
  184.7 7.3 fusion.3
  192.0 18.8 %collective-permute-done.1 = f32[192,1152]{1,0:T(8,128)S(1)} collective-permute-done((f32[192,1152]{1,0:T(8,128)S(1)}, f32[192,1152]{1,0:T(8,128)S(1)}, u32[]{:S(2)}, u32[]{:S(2)}) %collective-permute-start.1) | collective-permute-done | bytes 884768 | tf_op jit(solution)/shard_map/ppermute | solution.py:17
  211.2 14.7 %scatter_fusion = f32[192,6912]{0,1:T(8,128)} fusion(f32[192,6912]{0,1:T(8,128)} %fusion.3, s32[1152]{0:T(1024)S(1)} %compare_select_fusion.2, f32[1152,192]{1,0:T(8,128)S(1)} %copy.46), kind=kCustom, calls=%fused_computation.5 | custom fusion | flops 221184 | bytes 2658816 | tf_op jit(solution)/shard_map/scatter-add | solution.py:33
  225.9 7.0 fusion.6
  232.9 5.7 gather_fusion.2
  240.3 8.4 %collective-permute-done.2 = bf16[192,1152]{1,0:T(8,128)(2,1)S(1)} collective-permute-done((bf16[192,1152]{1,0:T(8,128)(2,1)S(1)}, bf16[192,1152]{1,0:T(8,128)(2,1)S(1)}, u32[]{:S(2)}, u32[]{:S(2)}) %collective-permute-start.2) | collective-permute-done | bytes 442400 | tf_op jit(solution)/shard_map/ppermute | solution.py:17
  253.7 28.3 %gather_fusion.3 = bf16[10976,192]{1,0:T(8,128)(2,1)} fusion(bf16[192,8064]{0,1:T(8,128)(2,1)} %pad_maximum_fusion.1, s32[11264]{0:T(1024)S(1)} %pad_clamp_fusion), kind=kCustom, calls=%fused_computation.3 | custom fusion | bytes 8473472 | tf_op jit(solution)/shard_map/gather | solution.py:25
  282.0 7.5 %copy.49 = bf16[10976,192]{0,1:T(8,128)(2,1)} copy(bf16[10976,192]{1,0:T(8,128)(2,1)} %gather_fusion.3) | data formatting | bytes 8429568 | tf_op jit(solution)/shard_map/gather | solution.py:25
  289.5 12.8 %reshape.71 = bf16[32,343,192]{1,0,2:T(8,128)(2,1)} reshape(bf16[10976,192]{0,1:T(8,128)(2,1)} %copy.49) | data formatting | bytes 8429568 | tf_op jit(solution)/shard_map/gather | solution.py:25
  302.3 9.0 %fusion.8 = f32[192,32,343]{2,1,0:T(8,128)} fusion(bf16[32,343,192]{1,0,2:T(8,128)(2,1)} %reshape.71, bf16[343,343]{1,0:T(8,128)(2,1)S(1)} %copy-done), kind=kOutput, calls=%fused_computation.21 | convolution fusion | flops 1445670912 | bytes 12879650 | tf_op jit(solution)/shard_map/wca,ea->wce/dot_general | solution.py:26
  311.3 11.1 %reshape.91 = f32[192,10976]{1,0:T(8,128)} reshape(f32[192,32,343]{2,1,0:T(8,128)} %fusion.8) | data formatting | bytes 16859136 | tf_op jit(solution)/shard_map/reshape | solution.py:30
  322.3 10.6 %copy.52 = f32[10976,192]{1,0:T(8,128)} copy(f32[10976,192]{0,1:T(8,128)} %bitcast.31) | data formatting | bytes 16859136 | tf_op jit(solution)/shard_map/reshape | solution.py:30
  332.9 59.1 %scatter_custom_fusion.2 = f32[192,8064]{0,1:T(8,128)} fusion(s32[10976]{0:T(1024)S(1)} %fusion.35, f32[10976,192]{1,0:T(8,128)} %copy.52, f32[]{:T(128)} %constant.14.clone.1), kind=kCustom, calls=%fused_computation.27 | custom fusion | flops 2107392 | bytes 6193664 | tf_op jit(solution)/shard_map/scatter-add | solution.py:30
  394.1 7.3 fusion
  401.4 16.3 %collective-permute-done.3 = f32[192,1152]{1,0:T(8,128)S(1)} collective-permute-done((f32[192,1152]{1,0:T(8,128)S(1)}, f32[192,1152]{1,0:T(8,128)S(1)}, u32[]{:S(2)}, u32[]{:S(2)}) %collective-permute-start.3) | collective-permute-done | bytes 884768 | tf_op jit(solution)/shard_map/ppermute | solution.py:17
  418.1 14.7 %scatter_fusion.1 = f32[192,6912]{0,1:T(8,128)} fusion(f32[192,6912]{0,1:T(8,128)} %fusion, s32[1152]{0:T(1024)S(1)} %compare_select_fusion.2, f32[1152,192]{1,0:T(8,128)S(1)} %copy.54), kind=kCustom, calls=%fused_computation.7 | custom fusion | flops 221184 | bytes 2658816 | tf_op jit(solution)/shard_map/scatter-add | solution.py:33
  432.8 8.4 %fusion.7 = bf16[192,6912]{0,1:T(8,128)(2,1)} fusion(bf16[192,6912]{0,1:T(8,128)(2,1)} %copy.38, f32[192,6912]{0,1:T(8,128)} %scatter_fusion.1, bf16[192,6912]{0,1:T(8,128)(2,1)} %fusion.6), kind=kLoop, calls=%fused_computation.20 | loop fusion | flops 9289728 | bytes 13271040 | tf_op jit(solution)/shard_map/convert_element_type | solution.py:64
  441.2 5.6 copy.55
  447.1 16.2 %all-gather.2.cloned.1.call-done = bf16[384,6912]{1,0:T(8,128)(2,1)} async-done(((bf16[192,6912]{1,0:T(8,128)(2,1)}), bf16[384,6912]{1,0:T(8,128)(2,1)}) %all-gather.2.cloned.1.call-update) | async-done | bytes 5308432 | tf_op jit(solution)/shard_map/all_gather | solution.py:66
  463.4 4.9 fusion.16
  468.3 254.1 %all-reduce.2.cloned.1.call-done = f32[384,384]{1,0:T(8,128)} async-done(((f32[384,384]{1,0:T(8,128)}), f32[384,384]{1,0:T(8,128)}) %all-reduce.2.cloned.1.call-update) | async-done | bytes 589840 | tf_op jit(solution)/shard_map/psum | solution.py:73
  (47 shorter events, 33.8 us)
Async XLA Ops:
  6.5 86.1 %copy-start = (bf16[343,343]{1,0:T(8,128)(2,1)S(1)}, bf16[343,343]{1,0:T(8,128)(2,1)}, u32[]{:S(2)}) copy-start(bf16[343,343]{1,0:T(8,128)(2,1)} %param.6) | copy-start | bytes 705898
  6.5 23.7 %copy-start.2 = (s32[32,343]{1,0:T(8,128)S(1)}, s32[32,343]{1,0:T(8,128)}, u32[]{:S(2)}) copy-start(s32[32,343]{1,0:T(8,128)} %param.8) | copy-start | bytes 131716
  6.5 456.8 %all-gather.2.cloned.1.call-start = ((), (), s32[]{:S(2)}) async-start(), calls=%async_computation | async-start | bytes 7962624 | tf_op jit(solution)/shard_map/all_gather | solution.py:66
  18.8 20.3 %collective-permute-start = (bf16[192,1152]{1,0:T(8,128)(2,1)S(1)}, bf16[192,1152]{1,0:T(8,128)(2,1)S(1)}, u32[]{:S(2)}, u32[]{:S(2)}) collective-permute-start(bf16[192,1152]{1,0:T(8,128)(2,1)S(1)} %copy.37), channel_id=1, source_target_pairs={{0,254},{2,0},{4,2},{6,4},{8,6},{10,8},{12,10},{14,12},{16,14},{18... | collective-permute-start | bytes 1327112 | tf_op jit(solution)/shard_map/ppermute | solution.py:17
  123.3 61.4 %copy-start.3 = (f32[6912]{0:T(1024)S(1)}, f32[6912]{0:T(1024)}, u32[]{:S(2)}) copy-start(f32[6912]{0:T(1024)} %param.7) | copy-start | bytes 82948
  184.6 26.2 %collective-permute-start.1 = (f32[192,1152]{1,0:T(8,128)S(1)}, f32[192,1152]{1,0:T(8,128)S(1)}, u32[]{:S(2)}, u32[]{:S(2)}) collective-permute-start(f32[192,1152]{1,0:T(8,128)S(1)} %copy.45), channel_id=1, source_target_pairs={{0,2},{2,4},{4,6},{6,8},{8,10},{10,12},{12,14},{14,16},{16,18},{18... | collective-permute-start | bytes 2654216 | tf_op jit(solution)/shard_map/ppermute | solution.py:17
  238.9 9.9 %collective-permute-start.2 = (bf16[192,1152]{1,0:T(8,128)(2,1)S(1)}, bf16[192,1152]{1,0:T(8,128)(2,1)S(1)}, u32[]{:S(2)}, u32[]{:S(2)}) collective-permute-start(bf16[192,1152]{1,0:T(8,128)(2,1)S(1)} %copy.47), channel_id=1, source_target_pairs={{0,254},{2,0},{4,2},{6,4},{8,6},{10,8},{12,10},{14,12},{16,14},{18... | collective-permute-start | bytes 1327112 | tf_op jit(solution)/shard_map/ppermute | solution.py:17
  393.8 24.0 %collective-permute-start.3 = (f32[192,1152]{1,0:T(8,128)S(1)}, f32[192,1152]{1,0:T(8,128)S(1)}, u32[]{:S(2)}, u32[]{:S(2)}) collective-permute-start(f32[192,1152]{1,0:T(8,128)S(1)} %copy.53), channel_id=1, source_target_pairs={{0,2},{2,4},{4,6},{6,8},{8,10},{10,12},{12,14},{14,16},{16,18},{18... | collective-permute-start | bytes 2654216 | tf_op jit(solution)/shard_map/ppermute | solution.py:17
  446.8 275.6 %all-reduce.2.cloned.1.call-start = ((), (), s32[]{:S(2)}) async-start(), calls=%async_computation.1 | async-start | bytes 1179648 | tf_op jit(solution)/shard_map/psum | solution.py:73
  722.4 9.0 %copy-start.1 = (f32[384,384]{1,0:T(8,128)S(1)}, f32[384,384]{1,0:T(8,128)}, u32[]{:S(2)}) copy-start(f32[384,384]{1,0:T(8,128)} %all-reduce.2.cloned.1.call-done) | copy-start | bytes 1769476
  725.0 10.3 %slice-start = ((s8[5308416]{0:T(1024)(128)(4,1)}), s8[4194304]{0:T(1024)(128)(4,1)S(1)}, s32[]{:S(2)}) async-start(s8[5308416]{0:T(1024)(128)(4,1)} %bitcast.32), calls=%async_computation.2 | async-start | bytes 8388608
  730.1 5.2 slice-start.1
Sparse Core Ops, SparseCore 0:
  447.0 16.3 all-gather.1
  468.9 253.4 all-reduce.1

commit v2 on v1

v2 whole, which is shorter than its diff:
```python
import functools

import jax
import jax.numpy as jnp
from jax import lax
from jax.experimental import pallas as pl
from jax.experimental.pallas import tpu as pltpu
from jax.sharding import PartitionSpec as P

NS_STEPS = 3
LANES = 128
BATCH = 24

cheb_center = 3.0
cheb_half = 7.0
epsilon = 1e-06

VMEM = pltpu.VMEM
SMEM = pltpu.SMEM


def block(space):
    return pl.BlockSpec(memory_space=space)


def passed_along(value, axis, steps):
    count = lax.axis_size(axis)
    pairs = [(source, (source + steps) % count) for source in range(count)]
    return lax.ppermute(value, axis, pairs)


def even(start):
    return pl.ds(start, LANES, stride=2)


def tile_start(tile):
    return pl.multiple_of(tile * (2 * LANES), 2 * LANES)


def padded(value):
    return jnp.concatenate([value, jnp.zeros((value.shape[0], LANES - value.shape[1]), value.dtype)], axis=1)


def spread(compact, tile, width):
    rows = compact[pl.ds(pl.multiple_of(tile * LANES, LANES), LANES), :].astype(jnp.float32)
    return rows[:, :LANES], padded(rows[:, LANES:width])


def pair_row(ref, row):
    return ref[pl.ds(row, 2), :]


def gather_rows(source, target, index, base, count):
    for row in range(count):
        target[2 * row : 2 * row + 2, :] = pair_row(source, index[base + row])


def add_rows(total, addend, index, base, count):
    for first in range(0, count, BATCH):
        rows = range(first, min(first + BATCH, count))
        places = [index[base + row] for row in rows]
        sums = [pair_row(total, place) + addend[2 * row : 2 * row + 2, :] for place, row in zip(places, rows)]
        for place, value in zip(places, sums):
            total[pl.ds(place, 2), :] = value


def transpose_kernel(width, states, face, table, faces, held):
    tiles = states.shape[1] // LANES
    face_count = faces.shape[0]

    def one(tile, carry):
        nodes = pl.ds(pl.multiple_of(tile * LANES, LANES), LANES)
        low = states[:LANES, nodes].astype(jnp.float32)
        high = states[LANES:width, nodes].astype(jnp.float32)
        high = jnp.concatenate([high, jnp.zeros((2 * LANES - width, LANES), jnp.float32)], axis=0)
        start = tile_start(tile)
        table[even(start), :] = low.T
        table[even(start + 1), :] = high.T
        return carry

    lax.fori_loop(0, tiles, one, 0)

    def some_faces(tile, carry):
        gather_rows(table, held, face, tile * LANES, LANES)
        rows = pl.ds(pl.multiple_of(tile * LANES, LANES), LANES)
        faces[rows, :LANES] = held[even(0), :].astype(faces.dtype)
        faces[rows, LANES:width] = held[even(1), :][:, : width - LANES].astype(faces.dtype)
        return carry

    lax.fori_loop(0, face_count // LANES, some_faces, 0)


def start_sums(table, total, potential, owned, ghosts):
    def one(tile, carry):
        factor = jnp.broadcast_to(potential[pl.ds(tile, 1), :], (LANES, LANES)).T - cheb_center
        start = tile_start(tile)
        total[even(start), :] = factor * table[even(start), :]
        total[even(start + 1), :] = factor * table[even(start + 1), :]
        return carry

    lax.fori_loop(0, owned // LANES, one, 0)
    total[2 * owned :, :] = jnp.zeros((2 * ghosts, LANES), jnp.float32)


def apply_cells(table, total, kinetic, index, slots, held, product):
    depth = kinetic.shape[0]
    held[2 * slots :, :] = jnp.zeros((2 * (depth - slots), LANES), jnp.float32)

    def one(cell, carry):
        base = cell * slots
        gather_rows(table, held, index, base, slots)
        values = jnp.concatenate(
            [held[pl.ds(0, depth, stride=2), :], held[pl.ds(1, depth, stride=2), :]], axis=1
        ).astype(jnp.bfloat16)
        result = jnp.dot(kinetic[...], values, preferred_element_type=jnp.float32)
        product[pl.ds(0, depth, stride=2), :] = result[:, :LANES]
        product[pl.ds(1, depth, stride=2), :] = result[:, LANES:]
        add_rows(total, product, index, base, slots)
        return carry

    lax.fori_loop(0, index.shape[0] // slots, one, 0)


def give_ghosts(total, owned, out, width):
    def one(tile, carry):
        start = tile_start(tile) + 2 * owned
        rows = pl.ds(pl.multiple_of(tile * LANES, LANES), LANES)
        out[rows, :LANES] = total[even(start), :]
        out[rows, LANES:width] = total[even(start + 1), :][:, : width - LANES]
        return carry

    lax.fori_loop(0, out.shape[0] // LANES, one, 0)


def first_kernel(
    width, slots, states_table, ghosts, potential, kinetic, index, face, total, ghost_out, face_out,
    table, held, product, sem,
):
    owned = states_table.shape[0] // 2
    face_count = ghosts.shape[0]
    copy = pltpu.make_async_copy(states_table, table.at[pl.ds(0, 2 * owned), :], sem)
    copy.start()

    def fill(tile, carry):
        start = tile_start(tile) + 2 * owned
        low, high = spread(ghosts, tile, width)
        table[even(start), :] = low
        table[even(start + 1), :] = high
        return carry

    lax.fori_loop(0, face_count // LANES, fill, 0)
    copy.wait()
    start_sums(table, total, potential, owned, face_count)
    apply_cells(table, total, kinetic, index, slots, held, product)
    give_ghosts(total, owned, ghost_out, width)

    def some_faces(tile, carry):
        gather_rows(total, held, face, tile * LANES, LANES)
        rows = pl.ds(pl.multiple_of(tile * LANES, LANES), LANES)
        face_out[rows, :LANES] = held[even(0), :]
        face_out[rows, LANES:width] = held[even(1), :][:, : width - LANES]
        return carry

    lax.fori_loop(0, face_count // LANES, some_faces, 0)


def add_returned(total, returned, face, held, width):
    def one(tile, carry):
        low, high = spread(returned, tile, width)
        held[even(0), :] = low
        held[even(1), :] = high
        add_rows(total, held, face, tile * LANES, LANES)
        return carry

    lax.fori_loop(0, returned.shape[0] // LANES, one, 0)


def second_kernel(
    width, slots, first_total, returned, ghost_sums, potential, kinetic, index, face, total, ghost_out,
    table, held, product, sem,
):
    rows_all = first_total.shape[0]
    face_count = returned.shape[0]
    owned = rows_all // 2 - face_count
    copy = pltpu.make_async_copy(first_total, table, sem)
    copy.start()
    copy.wait()
    add_returned(table, returned, face, held, width)

    def fill(tile, carry):
        start = tile_start(tile) + 2 * owned
        low, high = spread(ghost_sums, tile, width)
        table[even(start), :] = table[even(start), :] + low
        table[even(start + 1), :] = table[even(start + 1), :] + high
        return carry

    lax.fori_loop(0, face_count // LANES, fill, 0)

    def scale(tile, carry):
        rows = pl.ds(tile_start(tile), 2 * LANES)
        table[rows, :] = (table[rows, :] / cheb_half).astype(jnp.bfloat16).astype(jnp.float32)
        return carry

    lax.fori_loop(0, rows_all // (2 * LANES), scale, 0)
    start_sums(table, total, potential, owned, face_count)
    apply_cells(table, total, kinetic, index, slots, held, product)
    give_ghosts(total, owned, ghost_out, width)


def last_kernel(width, total_in, states_table, returned, face, filtered, total, table, held, sems):
    owned = filtered.shape[0]
    copies = [
        pltpu.make_async_copy(total_in.at[pl.ds(0, 2 * owned), :], total, sems.at[0]),
        pltpu.make_async_copy(states_table, table, sems.at[1]),
    ]
    for copy in copies:
        copy.start()
    copies[0].wait()
    add_returned(total, returned, face, held, width)
    copies[1].wait()

    def one(tile, carry):
        start = tile_start(tile)
        rows = pl.ds(pl.multiple_of(tile * LANES, LANES), LANES)
        low = 2.0 * total[even(start), :] / cheb_half - table[even(start), :]
        high = 2.0 * total[even(start + 1), :] / cheb_half - table[even(start + 1), :]
        filtered[rows, :LANES] = low.astype(filtered.dtype)
        filtered[rows, LANES:width] = high[:, : width - LANES].astype(filtered.dtype)
        return carry

    lax.fori_loop(0, owned // LANES, one, 0)


def filter_states(states, kinetic, potential, cell_nodes, face_map):
    width, owned = states.shape
    cells, slots = cell_nodes.shape
    face_count = face_map.shape[0]
    depth = -(-slots // 16) * 16
    f32 = jnp.float32
    face = 2 * face_map
    index = 2 * cell_nodes.reshape(-1)
    potential = potential.reshape(-1, LANES)
    kinetic = jnp.pad(kinetic, ((0, depth - slots), (0, depth - slots)))
    rows_all = 2 * (owned + face_count)
    work = [VMEM((2 * depth, LANES), f32), VMEM((2 * depth, LANES), f32)]
    params = pltpu.CompilerParams(vmem_limit_bytes=40 << 20)

    table, faces = pl.pallas_call(
        functools.partial(transpose_kernel, width),
        name="transpose_states",
        out_shape=(
            jax.ShapeDtypeStruct((2 * owned, LANES), f32),
            jax.ShapeDtypeStruct((face_count, width), states.dtype),
        ),
        in_specs=[block(VMEM), block(SMEM)],
        out_specs=(block(VMEM), block(VMEM)),
        scratch_shapes=[VMEM((2 * LANES, LANES), f32)],
        compiler_params=params,
    )(states, face)
    ghosts = passed_along(faces, "brick", -1)
    compact = jax.ShapeDtypeStruct((face_count, width), f32)
    first, ghost_part, face_part = pl.pallas_call(
        functools.partial(first_kernel, width, slots),
        name="first_apply",
        out_shape=(jax.ShapeDtypeStruct((rows_all, LANES), f32), compact, compact),
        in_specs=[block(pl.ANY)] + [block(VMEM)] * 3 + [block(SMEM)] * 2,
        out_specs=(block(VMEM),) * 3,
        scratch_shapes=[VMEM((rows_all, LANES), f32)] + work + [pltpu.SemaphoreType.DMA],
        compiler_params=params,
    )(table, ghosts, potential, kinetic, index, face)
    returned = passed_along(ghost_part, "brick", 1)
    ghost_sums = passed_along(face_part, "brick", -1)
    second, ghost_part = pl.pallas_call(
        functools.partial(second_kernel, width, slots),
        name="second_apply",
        out_shape=(jax.ShapeDtypeStruct((rows_all, LANES), f32), compact),
        in_specs=[block(pl.ANY)] + [block(VMEM)] * 4 + [block(SMEM)] * 2,
        out_specs=(block(VMEM),) * 2,
        scratch_shapes=[VMEM((rows_all, LANES), f32)] + work + [pltpu.SemaphoreType.DMA],
        compiler_params=params,
    )(first, returned, ghost_sums, potential, kinetic, index, face)
    returned = passed_along(ghost_part, "brick", 1)
    return pl.pallas_call(
        functools.partial(last_kernel, width),
        name="finish_filter",
        out_shape=jax.ShapeDtypeStruct((owned, width), jnp.bfloat16),
        in_specs=[block(pl.ANY)] * 2 + [block(VMEM), block(SMEM)],
        out_specs=block(VMEM),
        scratch_shapes=[VMEM((2 * owned, LANES), f32)] * 2
        + [VMEM((2 * LANES, LANES), f32), pltpu.SemaphoreType.DMA((2,))],
        compiler_params=params,
    )(second, table, returned, face)


def newton_schulz(margin):
    total = margin.shape[0]
    scale = jnp.sqrt(jnp.sum(margin * margin) + epsilon)
    current = margin / scale
    row_ids = lax.broadcasted_iota(jnp.int32, (total, total), 0)
    column_ids = lax.broadcasted_iota(jnp.int32, (total, total), 1)
    three = 3.0 * (row_ids == column_ids).astype(jnp.float32)
    factor = three - current
    current = 0.5 * jnp.dot(factor, current, precision=lax.Precision.HIGHEST)
    inverse = 0.5 * factor
    for iteration in range(1, NS_STEPS):
        factor = three - jnp.dot(inverse, current, precision=lax.Precision.HIGHEST)
        if iteration < NS_STEPS - 1:
            current = 0.5 * jnp.dot(factor, current, precision=lax.Precision.HIGHEST)
        inverse = 0.5 * jnp.dot(factor, inverse, precision=lax.Precision.HIGHEST)
    return inverse


def local(states, kinetic, potential, cell_nodes, face_map):
    filtered = filter_states(states, kinetic, potential, cell_nodes, face_map)
    owned, width = filtered.shape
    every = lax.all_gather(filtered, "state", axis=1, tiled=True)
    side = lax.axis_index("state")
    half = owned // 2
    share = lax.dynamic_slice_in_dim(every, side * half, half, axis=0)
    partial = lax.dot_general(
        share, share, (((0,), (0,)), ((), ())), preferred_element_type=jnp.float32
    )
    margin = lax.psum(partial, ("brick", "state"))
    root = newton_schulz(margin)
    root_rows = lax.dynamic_slice_in_dim(root, side * width, width, axis=0)
    return lax.dot_general(
        root_rows.astype(jnp.bfloat16), every, (((1,), (1,)), ((), ())),
        preferred_element_type=jnp.float32,
    )


def solution(mesh):
    in_specs = (P("state", "brick"), P(), P("brick"), P("brick", None), P("brick"))
    out_specs = P("state", "brick")
    return jax.shard_map(local, mesh=mesh, in_specs=in_specs, out_specs=out_specs, check_vma=False)
```

time: 751 us -> 500 us (0.67)
  other arithmetic: 190 us -> 3.39 us
  local copies, waits for them, and re-layouts: 169 us -> 28.3 us
  Pallas kernels: 0 us -> 96.6 us
  matrix products: 37 us -> 18 us
    scatter-add x4 -> x0, other arithmetic: 148 us -> none  [the longest x2 119 us: apply_operator(): summed = jnp.zeros((width, owned + face_count), jnp.float32).at[:, cell_n...]
    gather x10 -> x0, local copies, waits for them, and re-layouts: 109 us -> none  [the longest x6 97.3 us: apply_operator(): gathered = extended[:, cell_nodes]]
    pallas_call x0 -> x4, Pallas kernels: none -> 96.6 us  [the longest x1 42.1 us: filter_states(): pl.pallas_call(functools.partial(second_kernel, width, slots), name='seco...]
    reshape x5 -> x0, local copies, waits for them, and re-layouts: 43.5 us -> none  [the longest x4 43.3 us: apply_operator(): products.reshape(width, -1)]
    dot_general x4 -> x2, matrix products: 26.8 us -> 8.85 us  [the longest x1 4.93 us: local(): lax.dot_general(share, share, (((0,), (0,)), ((), ())), preferred_element...]
    convert_element_type x2 -> x0, other arithmetic: 15.4 us -> none  [the longest x1 8.41 us: local(): filtered = (2.0 * (second - cheb_center * filtered_once.astype(jnp.float3...]
    unnamed x13 -> x22, local copies, waits for them, and re-layouts: 5.6 us -> 16.1 us
    concatenate x2 -> x0, other arithmetic: 9.33 us -> none  [apply_operator(): extended = jnp.concatenate([vector, ghost_cols], axis=1)]
  transfers between devices with their start and end apart: 6 -> 6, of which waited for: 6 -> 5; matrix products, arithmetic and copies ran while one was open for 2% -> 1% of each run, Pallas kernels for 0% -> 0%
where the time goes in v2:
time: 500 us; the launch traced here: 499 us
  waiting for transfers between devices  319 us (64%)
  Pallas kernels  96.6 us (19%)
  local copies, waits for them, and re-layouts  28.3 us (6%)
  starting transfers between devices  19.1 us (4%)
  matrix products  18 us (4%)
  between operations  14.3 us (3%)
    psum x1, waiting for transfers between devices, local(): margin = lax.psum(partial, ('brick', 'state'))  254 us
    ppermute x4, waiting for transfers between devices, passed_along(): return lax.ppermute(value, axis, pairs)  49.7 us
    pallas_call x1, Pallas kernels, filter_states(): pl.pallas_call(functools.partial(second_kernel, width, slots), name='seco...  42.1 us
    pallas_call x1, Pallas kernels, filter_states(): pl.pallas_call(functools.partial(first_kernel, width, slots), name='first...  40.3 us
    ppermute x4, starting transfers between devices, passed_along(): return lax.ppermute(value, axis, pairs)  18.9 us
    unnamed x22, local copies, waits for them, and re-layouts  16.1 us
    all_gather x1, waiting for transfers between devices, local(): every = lax.all_gather(filtered, 'state', axis=1, tiled=True)  15.7 us
  transfers between devices with their start and end apart: 6, of which 5 were waited for; matrix products, arithmetic and copies ran while one was open for 1% of the time, Pallas kernels for 0%

profile of v2, /device:TPU:1, one launch (start us, length us, event | category | flops | bytes accessed | tf_op | source)
XLA Modules:
  0.0 499.3 jit_solution(5237672219223144047)
XLA Ops:
  7.2 1.7 copy-done.5
  9.0 7.2 %transpose_states.1 = (f32[13824,128]{1,0:T(8,128)S(1)}, bf16[1152,192]{1,0:T(8,128)(2,1)S(1)}) custom-call(bf16[192,6912]{1,0:T(8,128)(2,1)S(1)} %copy-done.5, s32[1152]{0:T(1024)S(1)} %broadcast_multiply_fusion.1.face), custom_call_target="tpu_custom_call" | custom-call | tf_op jit(solution)/shard_map/transpose_states/pallas_call | solution.py:248
  16.3 2.9 copy-done
  19.4 11.1 %collective-permute-start = (bf16[1152,192]{0,1:T(8,128)(2,1)S(1)}, bf16[1152,192]{0,1:T(8,128)(2,1)S(1)}, u32[]{:S(2)}, u32[]{:S(2)}) collective-permute-start(bf16[1152,192]{0,1:T(8,128)(2,1)S(1)} %copy.6), channel_id=1, source_target_pairs={{0,254},{2,0},{4,2},{6,4},{8,6},{10,8},{12,10},{14,12},{16,14},{18... | collective-permute-start | bytes 1327112 | tf_op jit(solution)/shard_map/ppermute | solution.py:29
  32.5 6.9 %collective-permute-done = bf16[1152,192]{0,1:T(8,128)(2,1)S(1)} collective-permute-done((bf16[1152,192]{0,1:T(8,128)(2,1)S(1)}, bf16[1152,192]{0,1:T(8,128)(2,1)S(1)}, u32[]{:S(2)}, u32[]{:S(2)}) %collective-permute-start) | collective-permute-done | bytes 442400 | tf_op jit(solution)/shard_map/ppermute | solution.py:29
  39.7 3.0 copy-done.1
  42.7 40.3 %first_apply.1 = (f32[16128,128]{1,0:T(8,128)}, f32[1152,192]{1,0:T(8,128)S(1)}, f32[1152,192]{1,0:T(8,128)S(1)}) custom-call(f32[13824,128]{1,0:T(8,128)S(1)} %copy-done.1, bf16[1152,192]{1,0:T(8,128)(2,1)S(1)} %copy.7.ghosts, f32[54,128]{1,0:T(8,128)S(1)} %bitcast.10, bf16[352,352]{1,0:T(8,128)(2,1)S(1)} %pad.4.kinetic, s32[10976]{0:T(1024)S(1)} %mul.54.index, ...), custom_call_target="tpu_custom_call" | custom-call | tf_op jit(solution)/shard_map/first_apply/pallas_call | solution.py:262
  83.0 1.3 copy.8
  84.6 7.7 %collective-permute-start.2 = (f32[1152,192]{0,1:T(8,128)S(1)}, f32[1152,192]{0,1:T(8,128)}, u32[]{:S(2)}, u32[]{:S(2)}) collective-permute-start(f32[1152,192]{0,1:T(8,128)S(1)} %copy.9), channel_id=1, source_target_pairs={{0,254},{2,0},{4,2},{6,4},{8,6},{10,8},{12,10},{14,12},{16,14},{18... | collective-permute-start | bytes 2654216 | tf_op jit(solution)/shard_map/ppermute | solution.py:29
  92.3 18.3 %collective-permute-done.1 = f32[1152,192]{0,1:T(8,128)S(1)} collective-permute-done((f32[1152,192]{0,1:T(8,128)}, f32[1152,192]{0,1:T(8,128)S(1)}, u32[]{:S(2)}, u32[]{:S(2)}) %collective-permute-start.1) | collective-permute-done | bytes 884768 | tf_op jit(solution)/shard_map/ppermute | solution.py:29
  111.0 1.5 copy.11.ghost_sums
  112.5 42.1 %second_apply.1 = (f32[16128,128]{1,0:T(8,128)S(1)}, f32[1152,192]{1,0:T(8,128)S(1)}) custom-call(f32[16128,128]{1,0:T(8,128)} %get-tuple-element.14.first_total, f32[1152,192]{1,0:T(8,128)S(1)} %copy.10.returned, f32[1152,192]{1,0:T(8,128)S(1)} %copy.11.ghost_sums, f32[54,128]{1,0:T(8,128)S(1)} %bitcast.11, bf16[352,352]{1,0:T(8,128)(2,1)S(1)} %pad.4.kinetic, ...), custom_call_target="tpu_custom_call" | custom-call | tf_op jit(solution)/shard_map/second_apply/pallas_call | solution.py:273
  154.6 3.2 copy-done.3
  157.8 1.0 copy-done.6
  158.8 1.6 copy.12
  160.5 24.5 %collective-permute-done.3 = f32[1152,192]{0,1:T(8,128)S(1)} collective-permute-done((f32[1152,192]{0,1:T(8,128)S(1)}, f32[1152,192]{0,1:T(8,128)S(1)}, u32[]{:S(2)}, u32[]{:S(2)}) %collective-permute-start.3) | collective-permute-done | bytes 884768 | tf_op jit(solution)/shard_map/ppermute | solution.py:29
  185.0 1.4 copy.13.returned
  186.4 3.0 copy-done.2
  189.4 1.3 copy-done.4
  190.7 7.0 %finish_filter.1 = bf16[6912,192]{1,0:T(8,128)(2,1)S(1)} custom-call(f32[16128,128]{1,0:T(8,128)} %copy-done.3, f32[13824,128]{1,0:T(8,128)S(1)} %copy-done.2, f32[1152,192]{1,0:T(8,128)S(1)} %copy-done.4, s32[1152]{0:T(1024)S(1)} %broadcast_multiply_fusion.1.face), custom_call_target="tpu_custom_call" | custom-call | tf_op jit(solution)/shard_map/finish_filter/pallas_call | solution.py:283
  197.6 4.1 copy.14
  201.9 15.7 %all-gather.2.cloned.1.call-done = bf16[6912,384]{0,1:T(8,128)(2,1)} async-done(((bf16[6912,192]{0,1:T(8,128)(2,1)}), bf16[6912,384]{0,1:T(8,128)(2,1)}) %all-gather.2.cloned.1.call-update) | async-done | bytes 5308432 | tf_op jit(solution)/shard_map/all_gather | solution.py:316
  217.6 4.9 fusion
  222.6 254.1 %all-reduce.3.cloned.1.call-done = f32[384,384]{1,0:T(8,128)} async-done(((f32[384,384]{1,0:T(8,128)}), f32[384,384]{1,0:T(8,128)}) %all-reduce.3.cloned.1.call-update) | async-done | bytes 589840 | tf_op jit(solution)/shard_map/psum | solution.py:323
  476.6 1.9 multiply_reduce_fusion
  479.2 2.7 convolution_multiply_fusion.2
  482.0 1.3 convolution_subtract_fusion.1
  483.3 1.3 convolution_multiply_fusion
  484.6 1.3 convolution_multiply_fusion.1
  485.9 1.3 convolution_subtract_fusion
  487.2 1.3 fusion.28
  488.5 3.9 fusion.14
  (31 shorter events, 4.2 us)
Async XLA Ops:
  6.5 211.1 %all-gather.2.cloned.1.call-start = ((), (), s32[]{:S(2)}) async-start(), calls=%async_computation | async-start | bytes 7962624 | tf_op jit(solution)/shard_map/all_gather | solution.py:316
  7.2 1.7 copy-start.5
  9.0 30.7 %copy-start.7 = (f32[6912]{0:T(1024)S(1)}, f32[6912]{0:T(1024)}, u32[]{:S(2)}) copy-start(f32[6912]{0:T(1024)} %param.7) | copy-start | bytes 82948
  16.2 2.9 copy-start
  19.4 20.0 %collective-permute-start = (bf16[1152,192]{0,1:T(8,128)(2,1)S(1)}, bf16[1152,192]{0,1:T(8,128)(2,1)S(1)}, u32[]{:S(2)}, u32[]{:S(2)}) collective-permute-start(bf16[1152,192]{0,1:T(8,128)(2,1)S(1)} %copy.6), channel_id=1, source_target_pairs={{0,254},{2,0},{4,2},{6,4},{8,6},{10,8},{12,10},{14,12},{16,14},{18... | collective-permute-start | bytes 1327112 | tf_op jit(solution)/shard_map/ppermute | solution.py:29
  39.7 3.0 copy-start.1
  84.3 26.3 %collective-permute-start.1 = (f32[1152,192]{0,1:T(8,128)}, f32[1152,192]{0,1:T(8,128)S(1)}, u32[]{:S(2)}, u32[]{:S(2)}) collective-permute-start(f32[1152,192]{0,1:T(8,128)} %copy.8), channel_id=1, source_target_pairs={{0,2},{2,4},{4,6},{6,8},{8,10},{10,12},{12,14},{14,16},{16,18},{18... | collective-permute-start | bytes 2654216 | tf_op jit(solution)/shard_map/ppermute | solution.py:29
  84.6 26.3 %collective-permute-start.2 = (f32[1152,192]{0,1:T(8,128)S(1)}, f32[1152,192]{0,1:T(8,128)}, u32[]{:S(2)}, u32[]{:S(2)}) collective-permute-start(f32[1152,192]{0,1:T(8,128)S(1)} %copy.9), channel_id=1, source_target_pairs={{0,254},{2,0},{4,2},{6,4},{8,6},{10,8},{12,10},{14,12},{16,14},{18... | collective-permute-start | bytes 2654216 | tf_op jit(solution)/shard_map/ppermute | solution.py:29
  154.6 3.2 copy-start.3
  157.8 1.0 copy-start.6
  160.4 24.6 %collective-permute-start.3 = (f32[1152,192]{0,1:T(8,128)S(1)}, f32[1152,192]{0,1:T(8,128)S(1)}, u32[]{:S(2)}, u32[]{:S(2)}) collective-permute-start(f32[1152,192]{0,1:T(8,128)S(1)} %copy.12), channel_id=1, source_target_pairs={{0,2},{2,4},{4,6},{6,8},{8,10},{10,12},{12,14},{14,16},{16,18},{18... | collective-permute-start | bytes 2654216 | tf_op jit(solution)/shard_map/ppermute | solution.py:29
  186.4 3.0 copy-start.2
  189.4 1.3 copy-start.4
  201.7 274.9 %all-reduce.3.cloned.1.call-start = ((), (), s32[]{:S(2)}) async-start(), calls=%async_computation.1 | async-start | bytes 1179648 | tf_op jit(solution)/shard_map/psum | solution.py:323
  476.6 5.3 %copy-start.8 = (f32[384,384]{1,0:T(8,128)S(1)}, f32[384,384]{1,0:T(8,128)}, u32[]{:S(2)}) copy-start(f32[384,384]{1,0:T(8,128)} %all-reduce.3.cloned.1.call-done) | copy-start | bytes 1769476
  479.2 9.3 %slice-start = ((s8[5308416]{0:T(1024)(128)(4,1)}), s8[4194304]{0:T(1024)(128)(4,1)S(1)}, s32[]{:S(2)}) async-start(s8[5308416]{0:T(1024)(128)(4,1)} %bitcast.12), calls=%async_computation.2 | async-start | bytes 8388608
  483.3 5.2 %slice-start.1 = ((s8[5308416]{0:T(1024)(128)(4,1)}), s8[1114112]{0:T(1024)(128)(4,1)S(1)}, s32[]{:S(2)}) async-start(s8[5308416]{0:T(1024)(128)(4,1)} %bitcast.12), calls=%async_computation.3 | async-start | bytes 2228224
Sparse Core Ops, SparseCore 0:
  201.8 15.7 all-gather.1
  223.1 253.4 all-reduce.2

commit v3 on v2

--- a/solution.py
+++ b/solution.py
@@ -208,7 +208,7 @@
 
 
 def last_kernel(width, total_in, states_table, returned, face, filtered, total, table, held, sems):
-    owned = filtered.shape[0]
+    owned = filtered.shape[1]
     copies = [
         pltpu.make_async_copy(total_in.at[pl.ds(0, 2 * owned), :], total, sems.at[0]),
         pltpu.make_async_copy(states_table, table, sems.at[1]),
@@ -221,11 +221,11 @@
 
     def one(tile, carry):
         start = tile_start(tile)
-        rows = pl.ds(pl.multiple_of(tile * LANES, LANES), LANES)
+        nodes = pl.ds(pl.multiple_of(tile * LANES, LANES), LANES)
         low = 2.0 * total[even(start), :] / cheb_half - table[even(start), :]
         high = 2.0 * total[even(start + 1), :] / cheb_half - table[even(start + 1), :]
-        filtered[rows, :LANES] = low.astype(filtered.dtype)
-        filtered[rows, LANES:width] = high[:, : width - LANES].astype(filtered.dtype)
+        filtered[:LANES, nodes] = low.T.astype(filtered.dtype)
+        filtered[LANES:width, nodes] = high.T[: width - LANES, :].astype(filtered.dtype)
         return carry
 
     lax.fori_loop(0, owned // LANES, one, 0)
@@ -283,7 +283,7 @@
     return pl.pallas_call(
         functools.partial(last_kernel, width),
         name="finish_filter",
-        out_shape=jax.ShapeDtypeStruct((owned, width), jnp.bfloat16),
+        out_shape=jax.ShapeDtypeStruct((width, owned), jnp.bfloat16),
         in_specs=[block(pl.ANY)] * 2 + [block(VMEM), block(SMEM)],
         out_specs=block(VMEM),
         scratch_shapes=[VMEM((2 * owned, LANES), f32)] * 2
@@ -292,41 +292,228 @@
     )(second, table, returned, face)
 
 
-def newton_schulz(margin):
+X_SIZE, Y_SIZE, Z_SIZE = 4, 4, 8
+PLANE = X_SIZE * Y_SIZE
+MESH = pl.DeviceIdType.MESH
+EXACT = lax.Precision.HIGHEST
+CHUNK = 768
+
+
+def across(left, right):
+    return lax.dot_general(left, right, (((1,), (1,)), ((), ())), preferred_element_type=jnp.float32)
+
+
+def product_of(left, right):
+    return jnp.dot(left, right, precision=EXACT, preferred_element_type=jnp.float32)
+
+
+def unpack(packed):
+    corner = packed[128:192, :]
+    right = jnp.concatenate([corner.T, packed[288:352, 64:128]], axis=0)
+    square = jnp.concatenate([packed[:192, :], right], axis=1)
+    mixed = jnp.concatenate([packed[192:288, :], packed[288:384, :64]], axis=1)
+    return square, mixed
+
+
+def root_kernel(
+    own, other, root_own, root_other,
+    share, inbox, part, levels, own_all, other_all, square, mixed, current, inverse,
+    state_sems, send_sems, plane_sems, level_sems, gather_sems, pair_sems,
+):
+    brick, side = lax.axis_index("brick"), lax.axis_index("state")
+    width, owned = own.shape
+    half = width // 2
+    y, z, x = brick % Y_SIZE, (brick // Y_SIZE) % Z_SIZE, brick // (Y_SIZE * Z_SIZE)
+    place = x * Y_SIZE + y
+
+    def in_plane(step):
+        target = (place + step) % PLANE
+        return target, ((target // Y_SIZE) * Z_SIZE + z) * Y_SIZE + target % Y_SIZE
+
+    def in_line(step):
+        return (x * Z_SIZE + (z + step) % Z_SIZE) * Y_SIZE + y
+
+    barrier = pltpu.get_barrier_semaphore()
+    pl.semaphore_signal(barrier, inc=1, device_id=(brick, 1 - side), device_id_type=MESH)
+    for step in range(1, PLANE):
+        pl.semaphore_signal(barrier, inc=1, device_id=(in_plane(step)[1], side), device_id_type=MESH)
+    for step in range(1, Z_SIZE):
+        pl.semaphore_signal(barrier, inc=1, device_id=(in_line(step), side), device_id_type=MESH)
+    pl.semaphore_wait(barrier, PLANE + Z_SIZE - 1)
+
+    pieces = 3
+    piece = owned // pieces
+    states = []
+    for number in range(pieces):
+        columns = pl.ds(number * piece, piece)
+        copy = pltpu.make_async_remote_copy(
+            src_ref=own.at[:, columns], dst_ref=other.at[:, columns],
+            send_sem=state_sems.at[0, number], recv_sem=state_sems.at[1, number],
+            device_id=(brick, 1 - side), device_id_type=MESH,
+        )
+        copy.start()
+        states.append(copy)
+
+    square[...] = jnp.zeros_like(square)
+    mixed[...] = jnp.zeros_like(mixed)
+
+    def add_square(number, carry):
+        values = own[:, pl.ds(pl.multiple_of(number * CHUNK, CHUNK), CHUNK)]
+        square[...] += across(values, values)
+        return carry
+
+    lax.fori_loop(0, owned // CHUNK, add_square, 0)
+    for number, copy in enumerate(states):
+        copy.wait()
+
+        def add_mixed(step, carry):
+            columns = pl.ds(pl.multiple_of(number * piece + step * CHUNK, CHUNK), CHUNK)
+
+            @pl.when(side == 0)
+            def _():
+                mixed[...] += across(own[:half, columns], other[:, columns])
+
+            @pl.when(side == 1)
+            def _():
+                mixed[...] += across(other[half:, columns], own[:, columns])
+
+            return carry
+
+        lax.fori_loop(0, piece // CHUNK, add_mixed, 0)
+
+    share[:192, :] = square[:, :128]
+    share[192:288, :] = mixed[:, :128]
+    share[288:352, :] = jnp.concatenate([mixed[:64, 128:], square[128:, 128:]], axis=1)
+    share[352:384, :] = jnp.concatenate([mixed[64:, 128:], jnp.zeros((32, 64), jnp.float32)], axis=1)
+
+    rows = share.shape[0] // PLANE
+    copies = []
+    for step in range(1, PLANE):
+        target, chip = in_plane(step)
+        copy = pltpu.make_async_remote_copy(
+            src_ref=share.at[pl.ds(pl.multiple_of(target * rows, 8), rows), :], dst_ref=inbox.at[step - 1],
+            send_sem=send_sems.at[step - 1], recv_sem=plane_sems.at[step - 1],
+            device_id=(chip, side), device_id_type=MESH,
+        )
+        copy.start()
+        copies.append(copy)
+    value = share[pl.ds(pl.multiple_of(place * rows, 8), rows), :]
+    for copy in copies:
+        copy.wait()
+    for step in range(PLANE - 1):
+        value = value + inbox[step]
+    part[...] = value
+    levels[z] = value
+    copies = []
+    for step in range(1, Z_SIZE):
+        copy = pltpu.make_async_remote_copy(
+            src_ref=part, dst_ref=levels.at[z],
+            send_sem=send_sems.at[PLANE - 2 + step], recv_sem=level_sems.at[step - 1],
+            device_id=(in_line(step), side), device_id_type=MESH,
+        )
+        copy.start()
+        copies.append(copy)
+    for copy in copies:
+        copy.wait()
+    value = levels[0]
+    for step in range(1, Z_SIZE):
+        value = value + levels[step]
+    own_all[place] = value
+    copies = []
+    for step in range(1, PLANE):
+        copy = pltpu.make_async_remote_copy(
+            src_ref=own_all.at[place], dst_ref=own_all.at[place],
+            send_sem=send_sems.at[PLANE + Z_SIZE - 3 + step], recv_sem=gather_sems.at[step - 1],
+            device_id=(in_plane(step)[1], side), device_id_type=MESH,
+        )
+        copy.start()
+        copies.append(copy)
+    for copy in copies:
+        copy.wait()
+    swap = pltpu.make_async_remote_copy(
+        src_ref=own_all, dst_ref=other_all, send_sem=pair_sems.at[0], recv_sem=pair_sems.at[1],
+        device_id=(brick, 1 - side), device_id_type=MESH,
+    )
+    swap.start()
+    swap.wait()
+
+    mine = own_all[...].reshape(PLANE * rows, 128)
+    theirs = other_all[...].reshape(PLANE * rows, 128)
+    first, first_mixed = unpack(jnp.where(side == 0, mine, theirs))
+    second, second_mixed = unpack(jnp.where(side == 0, theirs, mine))
+    both = jnp.concatenate([first_mixed, second_mixed], axis=0)
+    margin = jnp.concatenate(
+        [jnp.concatenate([first, both], axis=1), jnp.concatenate([both.T, second], axis=1)], axis=0
+    )
+    scale = jnp.sqrt(jnp.sum(margin * margin, axis=(0, 1), keepdims=True) + epsilon)
     total = margin.shape[0]
-    scale = jnp.sqrt(jnp.sum(margin * margin) + epsilon)
-    current = margin / scale
     row_ids = lax.broadcasted_iota(jnp.int32, (total, total), 0)
     column_ids = lax.broadcasted_iota(jnp.int32, (total, total), 1)
-    three = 3.0 * (row_ids == column_ids).astype(jnp.float32)
-    factor = three - current
-    current = 0.5 * jnp.dot(factor, current, precision=lax.Precision.HIGHEST)
-    inverse = 0.5 * factor
-    for iteration in range(1, NS_STEPS):
-        factor = three - jnp.dot(inverse, current, precision=lax.Precision.HIGHEST)
-        if iteration < NS_STEPS - 1:
-            current = 0.5 * jnp.dot(factor, current, precision=lax.Precision.HIGHEST)
-        inverse = 0.5 * jnp.dot(factor, inverse, precision=lax.Precision.HIGHEST)
-    return inverse
+    three = jnp.where(row_ids == column_ids, 3.0, 0.0)
+    start = margin / scale
+    factor = three - start
+    current[...] = 0.5 * product_of(factor, start)
+    inverse[...] = 0.5 * factor
+    for step in range(1, NS_STEPS - 1):
+        factor = three - product_of(inverse[...], current[...])
+        current[...] = 0.5 * product_of(factor, current[...])
+        inverse[...] = 0.5 * product_of(factor, inverse[...])
+    mine = pl.ds(pl.multiple_of(side * width, 8), width)
+    row_ids = lax.broadcasted_iota(jnp.int32, (width, total), 0) + side * width
+    column_ids = lax.broadcasted_iota(jnp.int32, (width, total), 1)
+    factor = jnp.where(row_ids == column_ids, 3.0, 0.0) - product_of(inverse[mine, :], current[...])
+    root = (0.5 * product_of(factor, inverse[...])).astype(root_own.dtype)
+    left, right = root[:, :width], root[:, width:]
+    root_own[...] = jnp.where(side == 0, left, right)
+    root_other[...] = jnp.where(side == 0, right, left)
+
+
+def inverse_root(filtered):
+    width, owned = filtered.shape
+    f32 = jnp.float32
+    rows = 384 // PLANE
+    square = jax.ShapeDtypeStruct((width, width), jnp.bfloat16)
+    dma = pltpu.SemaphoreType.DMA
+    return pl.pallas_call(
+        root_kernel,
+        name="inverse_root",
+        out_shape=(jax.ShapeDtypeStruct((width, owned), filtered.dtype), square, square),
+        in_specs=[block(VMEM)],
+        out_specs=(block(VMEM),) * 3,
+        scratch_shapes=[
+            VMEM((384, 128), f32), VMEM((PLANE - 1, rows, 128), f32), VMEM((rows, 128), f32),
+            VMEM((Z_SIZE, rows, 128), f32), VMEM((PLANE, rows, 128), f32), VMEM((PLANE, rows, 128), f32),
+            VMEM((width, width), f32), VMEM((width // 2, width), f32),
+            VMEM((2 * width, 2 * width), f32), VMEM((2 * width, 2 * width), f32),
+            dma((2, 3)), dma((2 * PLANE + Z_SIZE - 3,)), dma((PLANE - 1,)), dma((Z_SIZE - 1,)),
+            dma((PLANE - 1,)), dma((2,)),
+        ],
+        compiler_params=pltpu.CompilerParams(
+            collective_id=0, has_side_effects=True, vmem_limit_bytes=32 << 20
+        ),
+    )(filtered)
+
+
+def rotate_kernel(own, other, root_own, root_other, out):
+    out[...] = jnp.dot(root_own[...], own[...], preferred_element_type=jnp.float32) + jnp.dot(
+        root_other[...], other[...], preferred_element_type=jnp.float32
+    )
 
 
 def local(states, kinetic, potential, cell_nodes, face_map):
     filtered = filter_states(states, kinetic, potential, cell_nodes, face_map)
-    owned, width = filtered.shape
-    every = lax.all_gather(filtered, "state", axis=1, tiled=True)
-    side = lax.axis_index("state")
-    half = owned // 2
-    share = lax.dynamic_slice_in_dim(every, side * half, half, axis=0)
-    partial = lax.dot_general(
-        share, share, (((0,), (0,)), ((), ())), preferred_element_type=jnp.float32
-    )
-    margin = lax.psum(partial, ("brick", "state"))
-    root = newton_schulz(margin)
-    root_rows = lax.dynamic_slice_in_dim(root, side * width, width, axis=0)
-    return lax.dot_general(
-        root_rows.astype(jnp.bfloat16), every, (((1,), (1,)), ((), ())),
-        preferred_element_type=jnp.float32,
-    )
+    width, owned = filtered.shape
+    other, root_own, root_other = inverse_root(filtered)
+    columns = pl.BlockSpec((width, CHUNK), lambda step: (0, step))
+    whole = pl.BlockSpec((width, width), lambda step: (0, 0))
+    return pl.pallas_call(
+        rotate_kernel,
+        name="rotate",
+        grid=(owned // CHUNK,),
+        out_shape=jax.ShapeDtypeStruct((width, owned), jnp.float32),
+        in_specs=[columns, columns, whole, whole],
+        out_specs=columns,
+    )(filtered, other, root_own, root_other)
 
 
 def solution(mesh):

time: 500 us -> 254 us (0.51)
  waiting for transfers between devices: 319 us -> 57.1 us
  Pallas kernels: 96.6 us -> 150 us
  matrix products: 18 us -> 0 us
  between operations: 14.3 us -> 0.17 us
    psum x1 -> x0, waiting for transfers between devices: 254 us -> none  [local(): margin = lax.psum(partial, ('brick', 'state'))]
    pallas_call x0 -> x2, Pallas kernels: none -> 47.2 us  [the longest x1 38.3 us: inverse_root(): pl.pallas_call(root_kernel, name='inverse_root', out_shape=(jax.ShapeDtyp...]
    dot_general x8 -> x0, matrix products: 18 us -> none  [the longest x1 4.93 us: local(): lax.dot_general(share, share, (((0,), (0,)), ((), ())), preferred_element...]
    all_gather x1 -> x0, waiting for transfers between devices: 15.7 us -> none  [local(): every = lax.all_gather(filtered, 'state', axis=1, tiled=True)]
    ppermute x4, waiting for transfers between devices: 49.7 us -> 57.1 us  [passed_along(): return lax.ppermute(value, axis, pairs)]
    unnamed x22 -> x28, local copies, waits for them, and re-layouts: 16.1 us -> 19 us
  transfers between devices with their start and end apart: 6 -> 4, of which waited for: 5 -> 4; matrix products, arithmetic and copies ran while one was open for 1% -> 0% of each run, Pallas kernels for 0% -> 0%
where the time goes in v3:
time: 254 us; the launch traced here: 253 us
  Pallas kernels  150 us (59%)
  waiting for transfers between devices  57.1 us (22%)
  local copies, waits for them, and re-layouts  26.2 us (10%)
  starting transfers between devices  19.1 us (8%)
    ppermute x4, waiting for transfers between devices, passed_along(): return lax.ppermute(value, axis, pairs)  57.1 us
    pallas_call x1, Pallas kernels, filter_states(): pl.pallas_call(functools.partial(second_kernel, width, slots), name='seco...  43.6 us
    pallas_call x1, Pallas kernels, filter_states(): pl.pallas_call(functools.partial(first_kernel, width, slots), name='first...  41.2 us
    pallas_call x1, Pallas kernels, inverse_root(): pl.pallas_call(root_kernel, name='inverse_root', out_shape=(jax.ShapeDtyp...  38.3 us
    ppermute x4, starting transfers between devices, passed_along(): return lax.ppermute(value, axis, pairs)  19.1 us
    unnamed x28, local copies, waits for them, and re-layouts  19 us
    pallas_call x1, Pallas kernels, filter_states(): pl.pallas_call(functools.partial(last_kernel, width), name='finish_filter...  10.9 us
    pallas_call x1, Pallas kernels, local(): pl.pallas_call(rotate_kernel, name='rotate', grid=(owned // CHUNK,), out_...  8.85 us
  transfers between devices with their start and end apart: 4, of which 4 were waited for; matrix products, arithmetic and copies ran while one was open for 0% of the time, Pallas kernels for 0%

profile of v3, /device:TPU:1, one launch (start us, length us, event | category | flops | bytes accessed | tf_op | source)
XLA Modules:
  0.0 253.4 jit_solution(7491693840439200073)
XLA Ops:
  0.0 0.7 broadcast_multiply_fusion.1.face
  0.7 1.7 copy-done.6
  2.5 7.2 %transpose_states.1 = (f32[13824,128]{1,0:T(8,128)S(1)}, bf16[1152,192]{1,0:T(8,128)(2,1)S(1)}) custom-call(bf16[192,6912]{1,0:T(8,128)(2,1)S(1)} %copy-done.6, s32[1152]{0:T(1024)S(1)} %broadcast_multiply_fusion.1.face), custom_call_target="tpu_custom_call" | custom-call | tf_op jit(solution)/shard_map/transpose_states/pallas_call | solution.py:248
  9.7 2.9 %copy-done = f32[13824,128]{1,0:T(8,128)} copy-done((f32[13824,128]{1,0:T(8,128)}, f32[13824,128]{1,0:T(8,128)S(1)}, u32[]{:S(2)}) %copy-start) | copy-done | bytes 7077912
  12.6 0.3 copy.6
  12.9 11.1 %collective-permute-start = (bf16[1152,192]{0,1:T(8,128)(2,1)S(1)}, bf16[1152,192]{0,1:T(8,128)(2,1)S(1)}, u32[]{:S(2)}, u32[]{:S(2)}) collective-permute-start(bf16[1152,192]{0,1:T(8,128)(2,1)S(1)} %copy.6), channel_id=1, source_target_pairs={{0,254},{2,0},{4,2},{6,4},{8,6},{10,8},{12,10},{14,12},{16,14},{18... | collective-permute-start | bytes 1327112 | tf_op jit(solution)/shard_map/ppermute | solution.py:29
  24.2 8.7 %collective-permute-done = bf16[1152,192]{0,1:T(8,128)(2,1)S(1)} collective-permute-done((bf16[1152,192]{0,1:T(8,128)(2,1)S(1)}, bf16[1152,192]{0,1:T(8,128)(2,1)S(1)}, u32[]{:S(2)}, u32[]{:S(2)}) %collective-permute-start) | collective-permute-done | bytes 442400 | tf_op jit(solution)/shard_map/ppermute | solution.py:29
  32.8 0.2 copy.7.ghosts
  33.1 3.0 %copy-done.1 = f32[13824,128]{1,0:T(8,128)S(1)} copy-done((f32[13824,128]{1,0:T(8,128)S(1)}, f32[13824,128]{1,0:T(8,128)}, u32[]{:S(2)}) %copy-start.1) | copy-done | bytes 7077912
  36.1 41.2 %first_apply.1 = (f32[16128,128]{1,0:T(8,128)}, f32[1152,192]{1,0:T(8,128)S(1)}, f32[1152,192]{1,0:T(8,128)S(1)}) custom-call(f32[13824,128]{1,0:T(8,128)S(1)} %copy-done.1, bf16[1152,192]{1,0:T(8,128)(2,1)S(1)} %copy.7.ghosts, f32[54,128]{1,0:T(8,128)S(1)} %bitcast.1, bf16[352,352]{1,0:T(8,128)(2,1)S(1)} %pad.4.kinetic, s32[10976]{0:T(1024)S(1)} %mul.18.index, ...), custom_call_target="tpu_custom_call" | custom-call | tf_op jit(solution)/shard_map/first_apply/pallas_call | solution.py:262
  77.3 1.3 copy.9
  78.6 7.6 %collective-permute-start.2 = (f32[1152,192]{0,1:T(8,128)}, f32[1152,192]{0,1:T(8,128)S(1)}, u32[]{:S(2)}, u32[]{:S(2)}) collective-permute-start(f32[1152,192]{0,1:T(8,128)} %copy.9), channel_id=1, source_target_pairs={{0,254},{2,0},{4,2},{6,4},{8,6},{10,8},{12,10},{14,12},{16,14},{18... | collective-permute-start | bytes 2654216 | tf_op jit(solution)/shard_map/ppermute | solution.py:29
  86.2 0.3 copy.8
  86.7 17.3 %collective-permute-done.2 = f32[1152,192]{0,1:T(8,128)S(1)} collective-permute-done((f32[1152,192]{0,1:T(8,128)}, f32[1152,192]{0,1:T(8,128)S(1)}, u32[]{:S(2)}, u32[]{:S(2)}) %collective-permute-start.2) | collective-permute-done | bytes 884768 | tf_op jit(solution)/shard_map/ppermute | solution.py:29
  104.0 0.4 copy.11.ghost_sums
  104.4 7.2 %collective-permute-done.1 = f32[1152,192]{0,1:T(8,128)} collective-permute-done((f32[1152,192]{0,1:T(8,128)S(1)}, f32[1152,192]{0,1:T(8,128)}, u32[]{:S(2)}, u32[]{:S(2)}) %collective-permute-start.1) | collective-permute-done | bytes 884768 | tf_op jit(solution)/shard_map/ppermute | solution.py:29
  111.6 1.5 copy.10.returned
  113.1 43.6 %second_apply.1 = (f32[16128,128]{1,0:T(8,128)S(1)}, f32[1152,192]{1,0:T(8,128)S(1)}) custom-call(f32[16128,128]{1,0:T(8,128)} %get-tuple-element.17.first_total, f32[1152,192]{1,0:T(8,128)S(1)} %copy.10.returned, f32[1152,192]{1,0:T(8,128)S(1)} %copy.11.ghost_sums, f32[54,128]{1,0:T(8,128)S(1)} %bitcast.2, bf16[352,352]{1,0:T(8,128)(2,1)S(1)} %pad.4.kinetic, ...), custom_call_target="tpu_custom_call" | custom-call | tf_op jit(solution)/shard_map/second_apply/pallas_call | solution.py:273
  156.7 3.2 %copy-done.4 = f32[16128,128]{1,0:T(8,128)} copy-done((f32[16128,128]{1,0:T(8,128)}, f32[16128,128]{1,0:T(8,128)S(1)}, u32[]{:S(2)}) %copy-start.4) | copy-done | bytes 8257560
  159.9 1.0 copy-done.8
  160.9 1.6 copy.12
  162.5 0.3 collective-permute-start.3
  162.8 23.9 %collective-permute-done.3 = f32[1152,192]{0,1:T(8,128)S(1)} collective-permute-done((f32[1152,192]{0,1:T(8,128)S(1)}, f32[1152,192]{0,1:T(8,128)S(1)}, u32[]{:S(2)}, u32[]{:S(2)}) %collective-permute-start.3) | collective-permute-done | bytes 884768 | tf_op jit(solution)/shard_map/ppermute | solution.py:29
  186.7 1.4 copy.13.returned
  188.1 3.0 %copy-done.2 = f32[13824,128]{1,0:T(8,128)S(1)} copy-done((f32[13824,128]{1,0:T(8,128)S(1)}, f32[13824,128]{1,0:T(8,128)}, u32[]{:S(2)}) %copy-start.2) | copy-done | bytes 7077912
  191.1 1.3 copy-done.5
  192.4 10.9 %finish_filter.1.own = bf16[192,6912]{1,0:T(8,128)(2,1)S(1)} custom-call(f32[16128,128]{1,0:T(8,128)} %copy-done.4, f32[13824,128]{1,0:T(8,128)S(1)} %copy-done.2, f32[1152,192]{1,0:T(8,128)S(1)} %copy-done.5, s32[1152]{0:T(1024)S(1)} %broadcast_multiply_fusion.1.face), custom_call_target="tpu_custom_call" | custom-call | tf_op jit(solution)/shard_map/finish_filter/pallas_call | solution.py:283
  203.4 38.3 %inverse_root.1 = (bf16[192,6912]{1,0:T(8,128)(2,1)S(1)}, bf16[192,192]{1,0:T(8,128)(2,1)S(1)}, bf16[192,192]{1,0:T(8,128)(2,1)S(1)}) custom-call(bf16[192,6912]{1,0:T(8,128)(2,1)S(1)} %finish_filter.1.own), custom_call_target="tpu_custom_call" | custom-call | tf_op jit(solution)/shard_map/inverse_root/pallas_call | solution.py:477
  241.7 1.6 copy-done.7
  243.3 0.6 copy-done.10
  243.9 0.6 copy-done.11
  244.5 8.9 %rotate.1 = f32[192,6912]{1,0:T(8,128)} custom-call(bf16[192,6912]{1,0:T(8,128)(2,1)} %copy-done.3, bf16[192,6912]{1,0:T(8,128)(2,1)} %copy-done.7, bf16[192,192]{1,0:T(8,128)(2,1)} %copy-done.10, bf16[192,192]{1,0:T(8,128)(2,1)} %copy-done.11), custom_call_target="tpu_custom_call" | custom-call | tf_op jit(solution)/shard_map/rotate/pallas_call | solution.py:509
  (22 shorter events, 0.3 us)
Async XLA Ops:
  0.7 1.7 copy-start.6
  2.4 21.5 %copy-start.13 = (s32[32,343]{1,0:T(8,128)S(1)}, s32[32,343]{1,0:T(8,128)}, u32[]{:S(2)}) copy-start(s32[32,343]{1,0:T(8,128)} %param.8) | copy-start | bytes 131716
  2.5 21.7 %copy-start.12 = (bf16[343,343]{1,0:T(8,128)(2,1)S(1)}, bf16[343,343]{1,0:T(8,128)(2,1)}, u32[]{:S(2)}) copy-start(bf16[343,343]{1,0:T(8,128)(2,1)} %param.6) | copy-start | bytes 705898
  2.5 30.6 %copy-start.9 = (f32[6912]{0:T(1024)S(1)}, f32[6912]{0:T(1024)}, u32[]{:S(2)}) copy-start(f32[6912]{0:T(1024)} %param.7) | copy-start | bytes 82948
  9.7 2.9 %copy-start = (f32[13824,128]{1,0:T(8,128)}, f32[13824,128]{1,0:T(8,128)S(1)}, u32[]{:S(2)}) copy-start(f32[13824,128]{1,0:T(8,128)S(1)} %get-tuple-element.15.states_table) | copy-start | bytes 21233668
  12.9 20.0 %collective-permute-start = (bf16[1152,192]{0,1:T(8,128)(2,1)S(1)}, bf16[1152,192]{0,1:T(8,128)(2,1)S(1)}, u32[]{:S(2)}, u32[]{:S(2)}) collective-permute-start(bf16[1152,192]{0,1:T(8,128)(2,1)S(1)} %copy.6), channel_id=1, source_target_pairs={{0,254},{2,0},{4,2},{6,4},{8,6},{10,8},{12,10},{14,12},{16,14},{18... | collective-permute-start | bytes 1327112 | tf_op jit(solution)/shard_map/ppermute | solution.py:29
  33.1 3.0 %copy-start.1 = (f32[13824,128]{1,0:T(8,128)S(1)}, f32[13824,128]{1,0:T(8,128)}, u32[]{:S(2)}) copy-start(f32[13824,128]{1,0:T(8,128)} %copy-done) | copy-start | bytes 21233668
  78.6 25.4 %collective-permute-start.2 = (f32[1152,192]{0,1:T(8,128)}, f32[1152,192]{0,1:T(8,128)S(1)}, u32[]{:S(2)}, u32[]{:S(2)}) collective-permute-start(f32[1152,192]{0,1:T(8,128)} %copy.9), channel_id=1, source_target_pairs={{0,254},{2,0},{4,2},{6,4},{8,6},{10,8},{12,10},{14,12},{16,14},{18... | collective-permute-start | bytes 2654216 | tf_op jit(solution)/shard_map/ppermute | solution.py:29
  86.6 25.0 %collective-permute-start.1 = (f32[1152,192]{0,1:T(8,128)S(1)}, f32[1152,192]{0,1:T(8,128)}, u32[]{:S(2)}, u32[]{:S(2)}) collective-permute-start(f32[1152,192]{0,1:T(8,128)S(1)} %copy.8), channel_id=1, source_target_pairs={{0,2},{2,4},{4,6},{6,8},{8,10},{10,12},{12,14},{14,16},{16,18},{18... | collective-permute-start | bytes 2654216 | tf_op jit(solution)/shard_map/ppermute | solution.py:29
  156.7 3.2 %copy-start.4 = (f32[16128,128]{1,0:T(8,128)}, f32[16128,128]{1,0:T(8,128)S(1)}, u32[]{:S(2)}) copy-start(f32[16128,128]{1,0:T(8,128)S(1)} %get-tuple-element.20.total_in) | copy-start | bytes 24772612
  159.9 1.0 copy-start.8
  162.5 24.2 %collective-permute-start.3 = (f32[1152,192]{0,1:T(8,128)S(1)}, f32[1152,192]{0,1:T(8,128)S(1)}, u32[]{:S(2)}, u32[]{:S(2)}) collective-permute-start(f32[1152,192]{0,1:T(8,128)S(1)} %copy.12), channel_id=1, source_target_pairs={{0,2},{2,4},{4,6},{6,8},{8,10},{10,12},{12,14},{14,16},{16,18},{18... | collective-permute-start | bytes 2654216 | tf_op jit(solution)/shard_map/ppermute | solution.py:29
  188.1 3.0 %copy-start.2 = (f32[13824,128]{1,0:T(8,128)S(1)}, f32[13824,128]{1,0:T(8,128)}, u32[]{:S(2)}) copy-start(f32[13824,128]{1,0:T(8,128)} %copy-done) | copy-start | bytes 21233668
  191.1 1.3 copy-start.5
  203.3 41.2 %copy-start.3 = (bf16[192,6912]{1,0:T(8,128)(2,1)}, bf16[192,6912]{1,0:T(8,128)(2,1)S(1)}, u32[]{:S(2)}) copy-start(bf16[192,6912]{1,0:T(8,128)(2,1)S(1)} %finish_filter.1.own) | copy-start | bytes 7962628
  241.7 1.6 copy-start.7
  243.3 0.6 copy-start.10
  243.9 0.6 copy-start.11

commit v4 on v3

v4 whole, which is shorter than its diff:
```python
import functools

import jax
import jax.numpy as jnp
from jax import lax
from jax.experimental import pallas as pl
from jax.experimental.pallas import tpu as pltpu
from jax.sharding import PartitionSpec as P

NS_STEPS = 3
LANES = 128
BATCH = 24
GROUP = 4
LIMIT = 24 << 20

cheb_center = 3.0
cheb_half = 7.0
epsilon = 1e-06

VMEM = pltpu.VMEM
SMEM = pltpu.SMEM


def block(space):
    return pl.BlockSpec(memory_space=space)


def passed_along(value, axis, steps):
    count = lax.axis_size(axis)
    pairs = [(source, (source + steps) % count) for source in range(count)]
    return lax.ppermute(value, axis, pairs)


def even(start):
    return pl.ds(start, LANES, stride=2)


def tile_start(tile):
    return pl.multiple_of(tile * (2 * LANES), 2 * LANES)


def padded(value):
    return jnp.concatenate([value, jnp.zeros((value.shape[0], LANES - value.shape[1]), value.dtype)], axis=1)


def packed_rows(faces):
    return faces * 3 // 2


def pack(out, tile, low, high):
    faces = out.shape[0] * 2 // 3
    lane = lax.broadcasted_iota(jnp.int32, (LANES // 2, LANES), 1)
    joined = jnp.where(lane < LANES // 2, high[: LANES // 2], pltpu.roll(high[LANES // 2 :], LANES // 2, axis=1))
    out[tile * LANES : (tile + 1) * LANES, :] = low.astype(out.dtype)
    out[faces + tile * LANES // 2 : faces + (tile + 1) * LANES // 2, :] = joined.astype(out.dtype)


def unpack_rows(ref, tile):
    faces = ref.shape[0] * 2 // 3
    low = ref[tile * LANES : (tile + 1) * LANES, :].astype(jnp.float32)
    joined = ref[faces + tile * LANES // 2 : faces + (tile + 1) * LANES // 2, :].astype(jnp.float32)
    return low, jnp.concatenate([joined, pltpu.roll(joined, LANES // 2, axis=1)], axis=0)


def pair_row(ref, row):
    return ref[pl.ds(row, 2), :]


def gather_rows(source, target, places):
    for row, place in enumerate(places):
        target[2 * row : 2 * row + 2, :] = pair_row(source, place())


def add_rows(total, addend, places):
    for first in range(0, len(places), BATCH):
        rows = range(first, min(first + BATCH, len(places)))
        at = [places[row]() for row in rows]
        sums = [pair_row(total, place) + addend[2 * row : 2 * row + 2, :] for place, row in zip(at, rows)]
        for place, value in zip(at, sums):
            total[pl.ds(place, 2), :] = value


def entries(index, count, *lead):
    start = lead[-1] if lead else 0
    return [functools.partial(lambda i: index[i], start + row) for row in range(count)]


def gather_faces(source, held, face, out):
    for tile in range(face.shape[0] // LANES):
        buffer = held.at[tile % 2]
        gather_rows(source, buffer, entries(face, LANES, tile * LANES))
        pack(out, tile, buffer[even(0), :], buffer[even(1), :])


def fill_table(width, states, table):
    def one(tile, carry):
        nodes = pl.ds(pl.multiple_of(tile * LANES, LANES), LANES)
        low = states[:LANES, nodes].astype(jnp.float32)
        high = states[LANES:width, nodes].astype(jnp.float32)
        high = jnp.concatenate([high, jnp.zeros((2 * LANES - width, LANES), jnp.float32)], axis=0)
        start = tile_start(tile)
        table[even(start), :] = low.T
        table[even(start + 1), :] = high.T
        return carry

    lax.fori_loop(0, states.shape[1] // LANES, one, 0, unroll=2)


def copy_rows(source, target, count):
    def take(tile, carry):
        rows = pl.ds(tile_start(tile), 2 * LANES)
        target[rows, :] = source[rows, :]
        return carry

    lax.fori_loop(0, count // (2 * LANES), take, 0)


def faces_kernel(width, states, face, faces, table, held):
    fill_table(width, states, table)
    gather_faces(table, held, face, faces)


def start_sums(table, total, potential, owned, ghosts):
    def one(tile, carry):
        factor = jnp.broadcast_to(potential[pl.ds(tile, 1), :], (LANES, LANES)).T - cheb_center
        start = tile_start(tile)
        total[even(start), :] = factor * table[even(start), :]
        total[even(start + 1), :] = factor * table[even(start + 1), :]
        return carry

    lax.fori_loop(0, owned // LANES, one, 0)
    total[2 * owned :, :] = jnp.zeros((2 * ghosts, LANES), jnp.float32)


def apply_cells(table, total, kinetic, index, slots, held, product, places, sems):
    depth = kinetic.shape[0]
    groups, cells, _ = index.shape
    for side in range(2):
        held[side, 2 * slots :, :] = jnp.zeros((2 * (depth - slots), LANES), jnp.float32)

    def fetch(group, side):
        return pltpu.make_async_copy(index.at[group], places.at[side], sems.at[side])

    def one_group(group, side):
        fetch(group, side).wait()
        fetch(jnp.minimum(group + 1, groups - 1), 1 - side).start()
        for cell in range(cells):
            at = [functools.partial(lambda i: places[side, cell, i], row) for row in range(slots)]
            values, result = held.at[cell % 2], product.at[cell % 2]
            gather_rows(table, values, at)
            operand = jnp.concatenate(
                [values[pl.ds(0, depth, stride=2), :], values[pl.ds(1, depth, stride=2), :]], axis=1
            ).astype(jnp.bfloat16)
            answer = jnp.dot(kinetic[...], operand, preferred_element_type=jnp.float32)
            result[pl.ds(0, depth, stride=2), :] = answer[:, :LANES]
            result[pl.ds(1, depth, stride=2), :] = answer[:, LANES:]
            add_rows(total, result, at)

    fetch(0, 0).start()

    def two_groups(step, carry):
        one_group(2 * step, 0)
        one_group(2 * step + 1, 1)
        return carry

    lax.fori_loop(0, groups // 2, two_groups, 0)
    fetch(groups - 1, groups % 2).wait()


def give_ghosts(total, owned, out):
    for tile in range(out.shape[0] * 2 // 3 // LANES):
        start = 2 * owned + tile * 2 * LANES
        pack(out, tile, total[even(start), :], total[even(start + 1), :])


def first_kernel(
    width, slots, states, ghosts, potential, kinetic, index, face, sums, ghost_out, face_out,
    table, total, held, product, places, sems,
):
    owned = states.shape[1]
    face_count = face.shape[0]
    fill_table(width, states, table)
    for tile in range(face_count // LANES):
        start = 2 * owned + tile * 2 * LANES
        low, high = unpack_rows(ghosts, tile)
        table[even(start), :] = low
        table[even(start + 1), :] = high
    start_sums(table, total, potential, owned, face_count)
    apply_cells(table, total, kinetic, index, slots, held, product, places, sems)
    give_ghosts(total, owned, ghost_out)
    gather_faces(total, held, face, face_out)
    copy_rows(total, sums, total.shape[0])


def add_returned(total, returned, face, held):
    for tile in range(face.shape[0] // LANES):
        low, high = unpack_rows(returned, tile)
        buffer = held.at[tile % 2]
        buffer[even(0), :] = low
        buffer[even(1), :] = high
        add_rows(total, buffer, entries(face, LANES, tile * LANES))


def second_kernel(
    owned, slots, given, returned, ghost_sums, potential, kinetic, index, face, sums, ghost_out,
    table, total, held, product, places, sems,
):
    face_count = face.shape[0]
    rows_all = table.shape[0]
    copy_rows(given, table, rows_all)
    add_returned(table, returned, face, held)
    for tile in range(face_count // LANES):
        start = 2 * owned + tile * 2 * LANES
        low, high = unpack_rows(ghost_sums, tile)
        table[even(start), :] = table[even(start), :] + low
        table[even(start + 1), :] = table[even(start + 1), :] + high

    def scale(tile, carry):
        rows = pl.ds(tile_start(tile), 2 * LANES)
        table[rows, :] = (table[rows, :] / cheb_half).astype(jnp.bfloat16).astype(jnp.float32)
        return carry

    lax.fori_loop(0, rows_all // (2 * LANES), scale, 0)
    start_sums(table, total, potential, owned, face_count)
    apply_cells(table, total, kinetic, index, slots, held, product, places, sems)
    give_ghosts(total, owned, ghost_out)
    copy_rows(total, sums, 2 * owned)


def last_kernel(width, given, states, returned, face, filtered, total, held):
    owned = filtered.shape[1]
    copy_rows(given, total, 2 * owned)
    add_returned(total, returned, face, held)

    def one(tile, carry):
        start = tile_start(tile)
        nodes = pl.ds(pl.multiple_of(tile * LANES, LANES), LANES)
        low = (2.0 * total[even(start), :] / cheb_half).T
        high = (2.0 * total[even(start + 1), :] / cheb_half).T[: width - LANES, :]
        filtered[:LANES, nodes] = (low - states[:LANES, nodes].astype(jnp.float32)).astype(filtered.dtype)
        filtered[LANES:width, nodes] = (high - states[LANES:width, nodes].astype(jnp.float32)).astype(filtered.dtype)
        return carry

    lax.fori_loop(0, owned // LANES, one, 0, unroll=2)


def filter_states(states, kinetic, potential, cell_nodes, face_map):
    width, owned = states.shape
    cells, slots = cell_nodes.shape
    face_count = face_map.shape[0]
    depth = -(-slots // 16) * 16
    f32 = jnp.float32
    face = 2 * face_map
    index = jnp.pad(2 * cell_nodes, ((0, 0), (0, 384 - slots))).reshape(-1, GROUP, 384)
    potential = potential.reshape(-1, LANES)
    kinetic = jnp.pad(kinetic, ((0, depth - slots), (0, depth - slots)))
    rows_all = 2 * (owned + face_count)
    field = jax.ShapeDtypeStruct((rows_all, LANES), f32)
    sums = jax.ShapeDtypeStruct((packed_rows(face_count), LANES), f32)
    table = VMEM((rows_all, LANES), f32)
    faces_held = VMEM((2, 2 * LANES, LANES), f32)
    work = [
        VMEM((2, 2 * depth, LANES), f32), VMEM((2, 2 * depth, LANES), f32),
        SMEM((2, GROUP, 384), jnp.int32), pltpu.SemaphoreType.DMA((2,)),
    ]
    params = pltpu.CompilerParams(vmem_limit_bytes=LIMIT)

    faces = pl.pallas_call(
        functools.partial(faces_kernel, width),
        name="gather_faces",
        out_shape=jax.ShapeDtypeStruct(sums.shape, states.dtype),
        in_specs=[block(VMEM), block(SMEM)],
        out_specs=block(VMEM),
        scratch_shapes=[VMEM((2 * owned, LANES), f32), faces_held],
        compiler_params=params,
    )(states, face)
    ghosts = passed_along(faces, "brick", -1)
    first, ghost_part, face_part = pl.pallas_call(
        functools.partial(first_kernel, width, slots),
        name="first_apply",
        out_shape=(field, sums, sums),
        in_specs=[block(VMEM)] * 4 + [block(pl.ANY), block(SMEM)],
        out_specs=(block(VMEM),) * 3,
        scratch_shapes=[table, table] + work,
        compiler_params=params,
    )(states, ghosts, potential, kinetic, index, face)
    returned = passed_along(ghost_part, "brick", 1)
    ghost_sums = passed_along(face_part, "brick", -1)
    second, ghost_part = pl.pallas_call(
        functools.partial(second_kernel, owned, slots),
        name="second_apply",
        out_shape=(jax.ShapeDtypeStruct((2 * owned, LANES), f32), sums),
        in_specs=[block(VMEM)] * 5 + [block(pl.ANY), block(SMEM)],
        out_specs=(block(VMEM),) * 2,
        scratch_shapes=[table, table] + work,
        compiler_params=params,
    )(first, returned, ghost_sums, potential, kinetic, index, face)
    returned = passed_along(ghost_part, "brick", 1)
    return pl.pallas_call(
        functools.partial(last_kernel, width),
        name="finish_filter",
        out_shape=jax.ShapeDtypeStruct((width, owned), jnp.bfloat16),
        in_specs=[block(VMEM)] * 3 + [block(SMEM)],
        out_specs=block(VMEM),
        scratch_shapes=[VMEM((2 * owned, LANES), f32), faces_held],
        compiler_params=params,
    )(second, states, returned, face)


X_SIZE, Y_SIZE, Z_SIZE = 4, 4, 8
PLANE = X_SIZE * Y_SIZE
MESH = pl.DeviceIdType.MESH
EXACT = lax.Precision.HIGHEST
CHUNK = 768


def across(left, right):
    return lax.dot_general(left, right, (((1,), (1,)), ((), ())), preferred_element_type=jnp.float32)


def product_of(left, right):
    return jnp.dot(left, right, precision=EXACT, preferred_element_type=jnp.float32)


def unpack(packed):
    corner = packed[128:192, :]
    right = jnp.concatenate([corner.T, packed[288:352, 64:128]], axis=0)
    square = jnp.concatenate([packed[:192, :], right], axis=1)
    mixed = jnp.concatenate([packed[192:288, :], packed[288:384, :64]], axis=1)
    return square, mixed


def root_kernel(
    own, every, root_rows,
    share, inbox, part, levels, own_all, other_all, square, mixed, current, inverse,
    state_sems, here_sem, send_sems, plane_sems, level_sems, gather_sems, pair_sems,
):
    brick, side = lax.axis_index("brick"), lax.axis_index("state")
    width, owned = own.shape
    half = width // 2
    y, z, x = brick % Y_SIZE, (brick // Y_SIZE) % Z_SIZE, brick // (Y_SIZE * Z_SIZE)
    place = x * Y_SIZE + y

    def in_plane(step):
        target = (place + step) % PLANE
        return target, ((target // Y_SIZE) * Z_SIZE + z) * Y_SIZE + target % Y_SIZE

    def in_line(step):
        return (x * Z_SIZE + (z + step) % Z_SIZE) * Y_SIZE + y

    barrier = pltpu.get_barrier_semaphore()
    pl.semaphore_signal(barrier, inc=1, device_id=(brick, 1 - side), device_id_type=MESH)
    for step in range(1, PLANE):
        pl.semaphore_signal(barrier, inc=1, device_id=(in_plane(step)[1], side), device_id_type=MESH)
    for step in range(1, Z_SIZE):
        pl.semaphore_signal(barrier, inc=1, device_id=(in_line(step), side), device_id_type=MESH)
    pl.semaphore_wait(barrier, PLANE + Z_SIZE - 1)

    pieces = 3
    piece = owned // pieces
    place_here = pl.ds(pl.multiple_of(side * width, 16), width)
    here = pltpu.make_async_copy(own, every.at[place_here, :], here_sem)
    here.start()
    states = []
    for number in range(pieces):
        columns = pl.ds(number * piece, piece)
        copy = pltpu.make_async_remote_copy(
            src_ref=own.at[:, columns], dst_ref=every.at[place_here, columns],
            send_sem=state_sems.at[0, number], recv_sem=state_sems.at[1, number],
            device_id=(brick, 1 - side), device_id_type=MESH,
        )
        copy.start()
        states.append(copy)

    square[...] = jnp.zeros_like(square)
    mixed[...] = jnp.zeros_like(mixed)

    def add_square(number, carry):
        values = own[:, pl.ds(pl.multiple_of(number * CHUNK, CHUNK), CHUNK)]
        square[...] += across(values, values)
        return carry

    lax.fori_loop(0, owned // CHUNK, add_square, 0)
    here.wait()
    some = pl.ds(pl.multiple_of(side * half, 16), half)
    for number, copy in enumerate(states):
        copy.wait()

        def add_mixed(step, carry):
            columns = pl.ds(pl.multiple_of(number * piece + step * CHUNK, CHUNK), CHUNK)
            mixed[...] += across(every[some, columns], every[width:, columns])
            return carry

        lax.fori_loop(0, piece // CHUNK, add_mixed, 0)

    share[:192, :] = square[:, :128]
    share[192:288, :] = mixed[:, :128]
    share[288:352, :] = jnp.concatenate([mixed[:64, 128:], square[128:, 128:]], axis=1)
    share[352:384, :] = jnp.concatenate([mixed[64:, 128:], jnp.zeros((32, 64), jnp.float32)], axis=1)

    rows = share.shape[0] // PLANE
    copies = []
    for step in range(1, PLANE):
        target, chip = in_plane(step)
        copy = pltpu.make_async_remote_copy(
            src_ref=share.at[pl.ds(pl.multiple_of(target * rows, 8), rows), :], dst_ref=inbox.at[step - 1],
            send_sem=send_sems.at[step - 1], recv_sem=plane_sems.at[step - 1],
            device_id=(chip, side), device_id_type=MESH,
        )
        copy.start()
        copies.append(copy)
    value = share[pl.ds(pl.multiple_of(place * rows, 8), rows), :]
    for copy in copies:
        copy.wait()
    for step in range(PLANE - 1):
        value = value + inbox[step]
    part[...] = value
    levels[z] = value
    copies = []
    for step in range(1, Z_SIZE):
        copy = pltpu.make_async_remote_copy(
            src_ref=part, dst_ref=levels.at[z],
            send_sem=send_sems.at[PLANE - 2 + step], recv_sem=level_sems.at[step - 1],
            device_id=(in_line(step), side), device_id_type=MESH,
        )
        copy.start()
        copies.append(copy)
    for copy in copies:
        copy.wait()
    value = levels[0]
    for step in range(1, Z_SIZE):
        value = value + levels[step]
    own_all[place] = value
    copies = []
    for step in range(1, PLANE):
        copy = pltpu.make_async_remote_copy(
            src_ref=own_all.at[place], dst_ref=own_all.at[place],
            send_sem=send_sems.at[PLANE + Z_SIZE - 3 + step], recv_sem=gather_sems.at[step - 1],
            device_id=(in_plane(step)[1], side), device_id_type=MESH,
        )
        copy.start()
        copies.append(copy)
    for copy in copies:
        copy.wait()
    swap = pltpu.make_async_remote_copy(
        src_ref=own_all, dst_ref=other_all, send_sem=pair_sems.at[0], recv_sem=pair_sems.at[1],
        device_id=(brick, 1 - side), device_id_type=MESH,
    )
    swap.start()
    swap.wait()

    mine = own_all[...].reshape(PLANE * rows, 128)
    theirs = other_all[...].reshape(PLANE * rows, 128)
    first, first_mixed = unpack(jnp.where(side == 0, mine, theirs))
    second, second_mixed = unpack(jnp.where(side == 0, theirs, mine))
    both = jnp.concatenate([first_mixed, second_mixed], axis=0)
    margin = jnp.concatenate(
        [jnp.concatenate([first, both], axis=1), jnp.concatenate([both.T, second], axis=1)], axis=0
    )
    scale = jnp.sqrt(jnp.sum(margin * margin, axis=(0, 1), keepdims=True) + epsilon)
    total = margin.shape[0]
    row_ids = lax.broadcasted_iota(jnp.int32, (total, total), 0)
    column_ids = lax.broadcasted_iota(jnp.int32, (total, total), 1)
    three = jnp.where(row_ids == column_ids, 3.0, 0.0)
    start = margin / scale
    factor = three - start
    current[...] = 0.5 * product_of(factor, start)
    inverse[...] = 0.5 * factor
    for step in range(1, NS_STEPS - 1):
        factor = three - product_of(inverse[...], current[...])
        current[...] = 0.5 * product_of(factor, current[...])
        inverse[...] = 0.5 * product_of(factor, inverse[...])
    mine = pl.ds(pl.multiple_of(side * width, 8), width)
    row_ids = lax.broadcasted_iota(jnp.int32, (width, total), 0) + side * width
    column_ids = lax.broadcasted_iota(jnp.int32, (width, total), 1)
    factor = jnp.where(row_ids == column_ids, 3.0, 0.0) - product_of(inverse[mine, :], current[...])
    root_rows[...] = (0.5 * product_of(factor, inverse[...])).astype(root_rows.dtype)


def inverse_root(filtered):
    width, owned = filtered.shape
    f32 = jnp.float32
    rows = 384 // PLANE
    dma = pltpu.SemaphoreType.DMA
    return pl.pallas_call(
        root_kernel,
        name="inverse_root",
        out_shape=(
            jax.ShapeDtypeStruct((2 * width, owned), filtered.dtype),
            jax.ShapeDtypeStruct((width, 2 * width), jnp.bfloat16),
        ),
        in_specs=[block(VMEM)],
        out_specs=(block(VMEM),) * 2,
        scratch_shapes=[
            VMEM((384, 128), f32), VMEM((PLANE - 1, rows, 128), f32), VMEM((rows, 128), f32),
            VMEM((Z_SIZE, rows, 128), f32), VMEM((PLANE, rows, 128), f32), VMEM((PLANE, rows, 128), f32),
            VMEM((width, width), f32), VMEM((width // 2, width), f32),
            VMEM((2 * width, 2 * width), f32), VMEM((2 * width, 2 * width), f32),
            dma((2, 3)), dma, dma((2 * PLANE + Z_SIZE - 3,)), dma((PLANE - 1,)), dma((Z_SIZE - 1,)),
            dma((PLANE - 1,)), dma((2,)),
        ],
        compiler_params=pltpu.CompilerParams(
            collective_id=0, has_side_effects=True, vmem_limit_bytes=32 << 20
        ),
    )(filtered)


def local(states, kinetic, potential, cell_nodes, face_map):
    filtered = filter_states(states, kinetic, potential, cell_nodes, face_map)
    every, root_rows = inverse_root(filtered)
    return jnp.dot(root_rows, every, preferred_element_type=jnp.float32)


def solution(mesh):
    in_specs = (P("state", "brick"), P(), P("brick"), P("brick", None), P("brick"))
    out_specs = P("state", "brick")
    return jax.shard_map(local, mesh=mesh, in_specs=in_specs, out_specs=out_specs, check_vma=False)
```

time: 254 us -> 191 us (0.75)
  Pallas kernels: 150 us -> 113 us
  local copies, waits for them, and re-layouts: 26.2 us -> 3.51 us
  waiting for transfers between devices: 57.1 us -> 49.8 us
  matrix products: 0 us -> 3.93 us
    pallas_call x3 -> x2, Pallas kernels: 59.7 us -> 36.1 us  [the longest x1 31.8 us: filter_states(): pl.pallas_call(functools.partial(second_kernel, owned, slots), name='seco...]
    unnamed x28 -> x6, local copies, waits for them, and re-layouts: 19 us -> 2.5 us
    pallas_call x1, Pallas kernels: 41.2 us -> 32.7 us  [filter_states(): pl.pallas_call(functools.partial(first_kernel, width, slots), name='first...]
    ppermute x4, waiting for transfers between devices: 57.1 us -> 49.8 us  [passed_along(): return lax.ppermute(value, axis, pairs)]
    pallas_call x1, Pallas kernels: 10.9 us -> 6.25 us  [filter_states(): pl.pallas_call(functools.partial(last_kernel, width), name='finish_filter...]
    dot_general x0 -> x1, matrix products: none -> 3.93 us  [local(): return jnp.dot(root_rows, every, preferred_element_type=jnp.float32)]
    ppermute x4 -> x0, local copies, waits for them, and re-layouts: 3.53 us -> none  [passed_along(): return lax.ppermute(value, axis, pairs)]
    pallas_call x4 -> x0, local copies, waits for them, and re-layouts: 3.49 us -> none  [the longest x1 1.62 us: filter_states(): pl.pallas_call(functools.partial(second_kernel, width, slots), name='seco...]
  transfers between devices with their start and end apart: 4 -> 4, of which waited for: 4 -> 3; matrix products, arithmetic and copies ran while one was open for 0% -> 1% of each run, Pallas kernels for 0% -> 0%
where the time goes in v4:
time: 191 us
  Pallas kernels  113 us (59%)
  waiting for transfers between devices  49.8 us (26%)
  starting transfers between devices  19.5 us (10%)
  matrix products  3.93 us (2%)
  local copies, waits for them, and re-layouts  3.51 us (2%)
    ppermute x4, waiting for transfers between devices, passed_along(): return lax.ppermute(value, axis, pairs)  49.8 us
    pallas_call x1, Pallas kernels, inverse_root(): pl.pallas_call(root_kernel, name='inverse_root', out_shape=(jax.ShapeDtyp...  37.8 us
    pallas_call x1, Pallas kernels, filter_states(): pl.pallas_call(functools.partial(first_kernel, width, slots), name='first...  32.7 us
    pallas_call x1, Pallas kernels, filter_states(): pl.pallas_call(functools.partial(second_kernel, owned, slots), name='seco...  31.8 us
    ppermute x4, starting transfers between devices, passed_along(): return lax.ppermute(value, axis, pairs)  19.5 us
    pallas_call x1, Pallas kernels, filter_states(): pl.pallas_call(functools.partial(last_kernel, width), name='finish_filter...  6.25 us
    pallas_call x1, Pallas kernels, filter_states(): pl.pallas_call(functools.partial(faces_kernel, width), name='gather_faces...  4.34 us
    dot_general x1, matrix products, local(): return jnp.dot(root_rows, every, preferred_element_type=jnp.float32)  3.93 us
  transfers between devices with their start and end apart: 4, of which 3 were waited for; matrix products, arithmetic and copies ran while one was open for 1% of the time, Pallas kernels for 0%

profile of v4, /device:TPU:1, one launch (start us, length us, event | category | flops | bytes accessed | tf_op | source)
XLA Modules:
  0.0 191.1 jit_solution(13609608427077976045)
XLA Ops:
  0.0 0.7 broadcast_multiply_fusion.1.face
  0.7 0.0 copy-start
  0.7 1.7 copy-done
  2.4 0.0 copy-start.1
  2.5 4.3 %gather_faces.1 = bf16[1728,128]{1,0:T(8,128)(2,1)S(1)} custom-call(bf16[192,6912]{1,0:T(8,128)(2,1)S(1)} %copy-done, s32[1152]{0:T(1024)S(1)} %broadcast_multiply_fusion.1.face), custom_call_target="tpu_custom_call" | custom-call | tf_op jit(solution)/shard_map/gather_faces/pallas_call | solution.py:268
  6.8 11.1 %collective-permute-start = (bf16[1728,128]{1,0:T(8,128)(2,1)S(1)}, bf16[1728,128]{1,0:T(8,128)(2,1)}, u32[]{:S(2)}, u32[]{:S(2)}) collective-permute-start(bf16[1728,128]{1,0:T(8,128)(2,1)S(1)} %gather_faces.1), channel_id=1, source_target_pairs={{0,254},{2,0},{4,2},{6,4},{8,6},{10,8},{12,10},{14,12},{16,14},{18... | collective-permute-start | bytes 1327112 | tf_op jit(solution)/shard_map/ppermute | solution.py:31
  17.9 0.8 broadcast_multiply_fusion
  18.7 1.0 pad.8.kinetic
  19.7 7.0 %collective-permute-done.ghosts = bf16[1728,128]{1,0:T(8,128)(2,1)} collective-permute-done((bf16[1728,128]{1,0:T(8,128)(2,1)S(1)}, bf16[1728,128]{1,0:T(8,128)(2,1)}, u32[]{:S(2)}, u32[]{:S(2)}) %collective-permute-start) | collective-permute-done | bytes 442400 | tf_op jit(solution)/shard_map/ppermute | solution.py:31
  26.8 0.0 copy-done.1
  26.8 0.0 copy-start.2
  26.8 0.7 copy-done.2
  27.5 32.7 %first_apply.1 = (f32[16128,128]{1,0:T(8,128)S(1)}, f32[1728,128]{1,0:T(8,128)S(1)}, f32[1728,128]{1,0:T(8,128)S(1)}) custom-call(bf16[192,6912]{1,0:T(8,128)(2,1)S(1)} %copy-done.1, bf16[1728,128]{1,0:T(8,128)(2,1)} %collective-permute-done.ghosts, f32[54,128]{1,0:T(8,128)S(1)} %bitcast.3, bf16[352,352]{1,0:T(8,128)(2,1)S(1)} %pad.8.kinetic, ...), custom_call_target="tpu_custom_call" | custom-call | tf_op jit(solution)/shard_map/first_apply/pallas_call | solution.py:278
  60.2 0.1 collective-permute-start.1
  60.3 8.0 %collective-permute-start.2 = (f32[1728,128]{1,0:T(8,128)S(1)}, f32[1728,128]{1,0:T(8,128)S(1)}, u32[]{:S(2)}, u32[]{:S(2)}) collective-permute-start(f32[1728,128]{1,0:T(8,128)S(1)} %get-tuple-element.14), channel_id=1, source_target_pairs={{0,254},{2,0},{4,2},{6,4},{8,6},{10,8},{12,10},{14,12},{16,14},{18... | collective-permute-start | bytes 2654216 | tf_op jit(solution)/shard_map/ppermute | solution.py:31
  68.3 18.2 %collective-permute-done.1.returned = f32[1728,128]{1,0:T(8,128)S(1)} collective-permute-done((f32[1728,128]{1,0:T(8,128)S(1)}, f32[1728,128]{1,0:T(8,128)S(1)}, u32[]{:S(2)}, u32[]{:S(2)}) %collective-permute-start.1) | collective-permute-done | bytes 884768 | tf_op jit(solution)/shard_map/ppermute | solution.py:31
  86.5 0.0 collective-permute-done.2.ghost_sums
  86.5 31.8 %second_apply.1 = (f32[13824,128]{1,0:T(8,128)S(1)}, f32[1728,128]{1,0:T(8,128)S(1)}) custom-call(f32[16128,128]{1,0:T(8,128)S(1)} %get-tuple-element.12.given, f32[1728,128]{1,0:T(8,128)S(1)} %collective-permute-done.1.returned, f32[1728,128]{1,0:T(8,128)S(1)} %collective-permute-done.2.ghost_sums, f32[54,128]{1,0:T(8,128)S(1)} %bitcast.4, ...), custom_call_target="tpu_custom_call" | custom-call | tf_op jit(solution)/shard_map/second_apply/pallas_call | solution.py:289
  118.3 0.3 collective-permute-start.3
  118.6 24.5 %collective-permute-done.3.returned = f32[1728,128]{1,0:T(8,128)S(1)} collective-permute-done((f32[1728,128]{1,0:T(8,128)S(1)}, f32[1728,128]{1,0:T(8,128)S(1)}, u32[]{:S(2)}, u32[]{:S(2)}) %collective-permute-start.3) | collective-permute-done | bytes 884768 | tf_op jit(solution)/shard_map/ppermute | solution.py:31
  143.1 6.2 %finish_filter.1.own = bf16[192,6912]{1,0:T(8,128)(2,1)S(1)} custom-call(f32[13824,128]{1,0:T(8,128)S(1)} %get-tuple-element.15.given, bf16[192,6912]{1,0:T(8,128)(2,1)S(1)} %copy-done.1, f32[1728,128]{1,0:T(8,128)S(1)} %collective-permute-done.3.returned, s32[1152]{0:T(1024)S(1)} %broadcast_multiply_fusion.1.face), custom_call_target="tpu_custom_call" | custom-call | tf_op jit(solution)/shard_map/finish_filter/pallas_call | solution.py:299
  149.4 37.8 %inverse_root.1 = (bf16[384,6912]{1,0:T(8,128)(2,1)S(1)}, bf16[192,384]{1,0:T(8,128)(2,1)S(1)}) custom-call(bf16[192,6912]{1,0:T(8,128)(2,1)S(1)} %finish_filter.1.own), custom_call_target="tpu_custom_call" | custom-call | tf_op jit(solution)/shard_map/inverse_root/pallas_call | solution.py:485
  187.2 3.9 %fusion = f32[192,6912]{1,0:T(8,128)} fusion(bf16[192,384]{1,0:T(8,128)(2,1)S(1)} %get-tuple-element.17, bf16[384,6912]{1,0:T(8,128)(2,1)S(1)} %get-tuple-element.18), kind=kOutput, calls=%fused_computation.2 | convolution fusion | flops 1019215872 | bytes 10764288 | tf_op jit(solution)/shard_map/dot_general | solution.py:511
  (2 shorter events, 0.0 us)
Async XLA Ops:
  0.7 1.7 copy-start
  2.4 24.3 %copy-start.1 = (bf16[192,6912]{1,0:T(8,128)(2,1)S(1)}, bf16[192,6912]{1,0:T(8,128)(2,1)}, u32[]{:S(2)}) copy-start(bf16[192,6912]{1,0:T(8,128)(2,1)} %states.5) | copy-start | bytes 7962628
  6.8 20.0 %collective-permute-start = (bf16[1728,128]{1,0:T(8,128)(2,1)S(1)}, bf16[1728,128]{1,0:T(8,128)(2,1)}, u32[]{:S(2)}, u32[]{:S(2)}) collective-permute-start(bf16[1728,128]{1,0:T(8,128)(2,1)S(1)} %gather_faces.1), channel_id=1, source_target_pairs={{0,254},{2,0},{4,2},{6,4},{8,6},{10,8},{12,10},{14,12},{16,14},{18... | collective-permute-start | bytes 1327112 | tf_op jit(solution)/shard_map/ppermute | solution.py:31
  26.8 0.7 copy-start.2
  60.2 26.3 %collective-permute-start.1 = (f32[1728,128]{1,0:T(8,128)S(1)}, f32[1728,128]{1,0:T(8,128)S(1)}, u32[]{:S(2)}, u32[]{:S(2)}) collective-permute-start(f32[1728,128]{1,0:T(8,128)S(1)} %get-tuple-element.13), channel_id=1, source_target_pairs={{0,2},{2,4},{4,6},{6,8},{8,10},{10,12},{12,14},{14,16},{16,18},{18... | collective-permute-start | bytes 2654216 | tf_op jit(solution)/shard_map/ppermute | solution.py:31
  60.3 26.2 %collective-permute-start.2 = (f32[1728,128]{1,0:T(8,128)S(1)}, f32[1728,128]{1,0:T(8,128)S(1)}, u32[]{:S(2)}, u32[]{:S(2)}) collective-permute-start(f32[1728,128]{1,0:T(8,128)S(1)} %get-tuple-element.14), channel_id=1, source_target_pairs={{0,254},{2,0},{4,2},{6,4},{8,6},{10,8},{12,10},{14,12},{16,14},{18... | collective-permute-start | bytes 2654216 | tf_op jit(solution)/shard_map/ppermute | solution.py:31
  118.3 24.8 %collective-permute-start.3 = (f32[1728,128]{1,0:T(8,128)S(1)}, f32[1728,128]{1,0:T(8,128)S(1)}, u32[]{:S(2)}, u32[]{:S(2)}) collective-permute-start(f32[1728,128]{1,0:T(8,128)S(1)} %get-tuple-element.16), channel_id=1, source_target_pairs={{0,2},{2,4},{4,6},{6,8},{8,10},{10,12},{12,14},{14,16},{16,18},{18... | collective-permute-start | bytes 2654216 | tf_op jit(solution)/shard_map/ppermute | solution.py:31

commit v5 on v4

--- a/solution.py
+++ b/solution.py
@@ -11,7 +11,7 @@
 LANES = 128
 BATCH = 24
 GROUP = 4
-LIMIT = 24 << 20
+LIMIT = 20 << 20
 
 cheb_center = 3.0
 cheb_half = 7.0
@@ -93,17 +93,35 @@
 
 
 def fill_table(width, states, table):
+    rows = lax.broadcasted_iota(jnp.int32, (LANES, LANES), 0)
+    columns = lax.broadcasted_iota(jnp.int32, (LANES, LANES), 1)
+    identity = jnp.where(rows == columns, 1.0, 0.0).astype(states.dtype)
+
     def one(tile, carry):
         nodes = pl.ds(pl.multiple_of(tile * LANES, LANES), LANES)
-        low = states[:LANES, nodes].astype(jnp.float32)
-        high = states[LANES:width, nodes].astype(jnp.float32)
-        high = jnp.concatenate([high, jnp.zeros((2 * LANES - width, LANES), jnp.float32)], axis=0)
+        values = jnp.concatenate(
+            [states[:, nodes], jnp.zeros((2 * LANES - width, LANES), states.dtype)], axis=0
+        )
+        turned = lax.dot_general(
+            identity, values, (((1,), (1,)), ((), ())), preferred_element_type=jnp.float32
+        )
         start = tile_start(tile)
-        table[even(start), :] = low.T
-        table[even(start + 1), :] = high.T
-        return carry
-
-    lax.fori_loop(0, states.shape[1] // LANES, one, 0, unroll=2)
+        table[even(start), :] = turned[:, :LANES]
+        table[even(start + 1), :] = turned[:, LANES:]
+        return carry
+
+    lax.fori_loop(0, states.shape[1] // LANES, one, 0, unroll=3)
+
+
+def spread_kernel(potential, factor):
+    def one(tile, carry):
+        value = jnp.broadcast_to(potential[pl.ds(tile, 1), :], (LANES, LANES)).T - cheb_center
+        start = tile_start(tile)
+        factor[even(start), :] = value
+        factor[even(start + 1), :] = value
+        return carry
+
+    lax.fori_loop(0, potential.shape[0], one, 0)
 
 
 def copy_rows(source, target, count):
@@ -120,15 +138,13 @@
     gather_faces(table, held, face, faces)
 
 
-def start_sums(table, total, potential, owned, ghosts):
+def start_sums(table, total, factor, owned, ghosts):
     def one(tile, carry):
-        factor = jnp.broadcast_to(potential[pl.ds(tile, 1), :], (LANES, LANES)).T - cheb_center
-        start = tile_start(tile)
-        total[even(start), :] = factor * table[even(start), :]
-        total[even(start + 1), :] = factor * table[even(start + 1), :]
-        return carry
-
-    lax.fori_loop(0, owned // LANES, one, 0)
+        rows = pl.ds(pl.multiple_of(tile * LANES, LANES), LANES)
+        total[rows, :] = factor[rows, :] * table[rows, :]
+        return carry
+
+    lax.fori_loop(0, 2 * owned // LANES, one, 0, unroll=2)
     total[2 * owned :, :] = jnp.zeros((2 * ghosts, LANES), jnp.float32)
 
 
@@ -252,7 +268,15 @@
     f32 = jnp.float32
     face = 2 * face_map
     index = jnp.pad(2 * cell_nodes, ((0, 0), (0, 384 - slots))).reshape(-1, GROUP, 384)
-    potential = potential.reshape(-1, LANES)
+    potential = pl.pallas_call(
+        spread_kernel,
+        name="spread_potential",
+        out_shape=jax.ShapeDtypeStruct((2 * owned, LANES), f32),
+        in_specs=[block(VMEM)],
+        out_specs=block(VMEM),
+        compiler_params=pltpu.CompilerParams(vmem_limit_bytes=LIMIT),
+        cost_estimate=pl.CostEstimate(flops=2 * owned * LANES, bytes_accessed=24 * owned * LANES, transcendentals=0),
+    )(potential.reshape(-1, LANES))
     kinetic = jnp.pad(kinetic, ((0, depth - slots), (0, depth - slots)))
     rows_all = 2 * (owned + face_count)
     field = jax.ShapeDtypeStruct((rows_all, LANES), f32)

time: 191 us -> 185 us (0.969)
  waiting for transfers between devices: 49.8 us -> 43.6 us
  local copies, waits for them, and re-layouts: 3.51 us -> 5.54 us
    ppermute x4, waiting for transfers between devices: 49.8 us -> 43.6 us  [passed_along(): return lax.ppermute(value, axis, pairs)]
    pallas_call x0 -> x1, Pallas kernels: none -> 5.45 us  [filter_states(): pl.pallas_call(spread_kernel, name='spread_potential', out_shape=jax.Shap...]
    pallas_call x1, Pallas kernels: 31.8 us -> 27.1 us  [filter_states(): pl.pallas_call(functools.partial(second_kernel, owned, slots), name='seco...]
    pallas_call x1, Pallas kernels: 32.7 us -> 29.4 us  [filter_states(): pl.pallas_call(functools.partial(first_kernel, width, slots), name='first...]
  transfers between devices with their start and end apart: 4 -> 4, of which waited for: 3 -> 2; matrix products, arithmetic and copies ran while one was open for 1% -> 2% of each run, Pallas kernels for 0% -> 3%
where the time goes in v5:
time: 185 us
  Pallas kernels  112 us (61%)
  waiting for transfers between devices  43.6 us (24%)
  starting transfers between devices  18.4 us (10%)
  local copies, waits for them, and re-layouts  5.54 us (3%)
  matrix products  3.96 us (2%)
    ppermute x4, waiting for transfers between devices, passed_along(): return lax.ppermute(value, axis, pairs)  43.6 us
    pallas_call x1, Pallas kernels, inverse_root(): pl.pallas_call(root_kernel, name='inverse_root', out_shape=(jax.ShapeDtyp...  37.5 us
    pallas_call x1, Pallas kernels, filter_states(): pl.pallas_call(functools.partial(first_kernel, width, slots), name='first...  29.4 us
    pallas_call x1, Pallas kernels, filter_states(): pl.pallas_call(functools.partial(second_kernel, owned, slots), name='seco...  27.1 us
    ppermute x4, starting transfers between devices, passed_along(): return lax.ppermute(value, axis, pairs)  18.4 us
    pallas_call x1, Pallas kernels, filter_states(): pl.pallas_call(functools.partial(last_kernel, width), name='finish_filter...  6.26 us
    pallas_call x1, Pallas kernels, filter_states(): pl.pallas_call(functools.partial(faces_kernel, width), name='gather_faces...  6.1 us
    pallas_call x1, Pallas kernels, filter_states(): pl.pallas_call(spread_kernel, name='spread_potential', out_shape=jax.Shap...  5.45 us
  transfers between devices with their start and end apart: 4, of which 2 were waited for; matrix products, arithmetic and copies ran while one was open for 2% of the time, Pallas kernels for 3%

profile of v5, /device:TPU:1, one launch (start us, length us, event | category | flops | bytes accessed | tf_op | source)
XLA Modules:
  0.0 184.9 jit_solution(8841253220193864265)
XLA Ops:
  0.0 0.7 broadcast_multiply_fusion.1.face
  0.7 0.0 copy-start
  0.7 1.7 copy-done
  2.4 0.0 copy-start.1
  2.5 6.1 %gather_faces.1 = bf16[1728,128]{1,0:T(8,128)(2,1)S(1)} custom-call(bf16[192,6912]{1,0:T(8,128)(2,1)S(1)} %copy-done, s32[1152]{0:T(1024)S(1)} %broadcast_multiply_fusion.1.face), custom_call_target="tpu_custom_call" | custom-call | tf_op jit(solution)/shard_map/gather_faces/pallas_call | solution.py:292
  8.5 11.1 %collective-permute-start = (bf16[1728,128]{1,0:T(8,128)(2,1)S(1)}, bf16[1728,128]{1,0:T(8,128)(2,1)S(1)}, u32[]{:S(2)}, u32[]{:S(2)}) collective-permute-start(bf16[1728,128]{1,0:T(8,128)(2,1)S(1)} %gather_faces.1), channel_id=1, source_target_pairs={{0,254},{2,0},{4,2},{6,4},{8,6},{10,8},{12,10},{14,12},{16,14},{18... | collective-permute-start | bytes 1327112 | tf_op jit(solution)/shard_map/ppermute | solution.py:31
  19.7 0.8 broadcast_multiply_fusion
  20.5 0.6 pad.9
  21.1 1.4 reshape.7.index
  22.5 0.0 copy-start.2
  22.5 1.0 pad.8.kinetic
  23.5 0.0 copy-start.3
  23.5 0.7 copy-done.3
  24.3 5.5 %spread_potential.1.potential = f32[13824,128]{1,0:T(8,128)S(1)} custom-call(f32[54,128]{1,0:T(8,128)S(1)} %bitcast.3), custom_call_target="tpu_custom_call" | custom-call | flops 1769472 | bytes 21233664 | tf_op jit(solution)/shard_map/spread_potential/pallas_call | solution.py:271
  29.7 0.0 collective-permute-done.ghosts
  29.7 0.0 copy-done.1
  29.7 0.0 copy-done.2
  29.8 29.4 %first_apply.1 = (f32[16128,128]{1,0:T(8,128)S(1)}, f32[1728,128]{1,0:T(8,128)S(1)}, f32[1728,128]{1,0:T(8,128)S(1)}) custom-call(bf16[192,6912]{1,0:T(8,128)(2,1)S(1)} %copy-done.1, bf16[1728,128]{1,0:T(8,128)(2,1)S(1)} %collective-permute-done.ghosts, f32[13824,128]{1,0:T(8,128)S(1)} %spread_potential.1.potential, bf16[352,352]{1,0:T(8,128)(2,1)S(1)} %pad.8.kinetic, ...), custom_call_target="tpu_custom_call" | custom-call | tf_op jit(solution)/shard_map/first_apply/pallas_call | solution.py:302
  59.2 0.1 collective-permute-start.1
  59.2 6.9 %collective-permute-start.2 = (f32[1728,128]{1,0:T(8,128)S(1)}, f32[1728,128]{1,0:T(8,128)S(1)}, u32[]{:S(2)}, u32[]{:S(2)}) collective-permute-start(f32[1728,128]{1,0:T(8,128)S(1)} %get-tuple-element.14), channel_id=1, source_target_pairs={{0,254},{2,0},{4,2},{6,4},{8,6},{10,8},{12,10},{14,12},{16,14},{18... | collective-permute-start | bytes 2654216 | tf_op jit(solution)/shard_map/ppermute | solution.py:31
  66.1 18.8 %collective-permute-done.1.returned = f32[1728,128]{1,0:T(8,128)S(1)} collective-permute-done((f32[1728,128]{1,0:T(8,128)S(1)}, f32[1728,128]{1,0:T(8,128)S(1)}, u32[]{:S(2)}, u32[]{:S(2)}) %collective-permute-start.1) | collective-permute-done | bytes 884768 | tf_op jit(solution)/shard_map/ppermute | solution.py:31
  84.9 0.0 collective-permute-done.2.ghost_sums
  84.9 27.1 %second_apply.1 = (f32[13824,128]{1,0:T(8,128)S(1)}, f32[1728,128]{1,0:T(8,128)S(1)}) custom-call(f32[16128,128]{1,0:T(8,128)S(1)} %get-tuple-element.12.given, f32[1728,128]{1,0:T(8,128)S(1)} %collective-permute-done.1.returned, f32[1728,128]{1,0:T(8,128)S(1)} %collective-permute-done.2.ghost_sums, f32[13824,128]{1,0:T(8,128)S(1)} %spread_potential.1.potential, ...), custom_call_target="tpu_custom_call" | custom-call | tf_op jit(solution)/shard_map/second_apply/pallas_call | solution.py:313
  112.0 0.3 collective-permute-start.3
  112.3 24.8 %collective-permute-done.3.returned = f32[1728,128]{1,0:T(8,128)S(1)} collective-permute-done((f32[1728,128]{1,0:T(8,128)S(1)}, f32[1728,128]{1,0:T(8,128)S(1)}, u32[]{:S(2)}, u32[]{:S(2)}) %collective-permute-start.3) | collective-permute-done | bytes 884768 | tf_op jit(solution)/shard_map/ppermute | solution.py:31
  137.1 6.3 %finish_filter.1.own = bf16[192,6912]{1,0:T(8,128)(2,1)S(1)} custom-call(f32[13824,128]{1,0:T(8,128)S(1)} %get-tuple-element.15.given, bf16[192,6912]{1,0:T(8,128)(2,1)S(1)} %copy-done.1, f32[1728,128]{1,0:T(8,128)S(1)} %collective-permute-done.3.returned, s32[1152]{0:T(1024)S(1)} %broadcast_multiply_fusion.1.face), custom_call_target="tpu_custom_call" | custom-call | tf_op jit(solution)/shard_map/finish_filter/pallas_call | solution.py:323
  143.4 37.5 %inverse_root.1 = (bf16[384,6912]{1,0:T(8,128)(2,1)S(1)}, bf16[192,384]{1,0:T(8,128)(2,1)S(1)}) custom-call(bf16[192,6912]{1,0:T(8,128)(2,1)S(1)} %finish_filter.1.own), custom_call_target="tpu_custom_call" | custom-call | tf_op jit(solution)/shard_map/inverse_root/pallas_call | solution.py:509
  180.9 4.0 %fusion = f32[192,6912]{1,0:T(8,128)} fusion(bf16[192,384]{1,0:T(8,128)(2,1)S(1)} %get-tuple-element.17, bf16[384,6912]{1,0:T(8,128)(2,1)S(1)} %get-tuple-element.18), kind=kOutput, calls=%fused_computation.2 | convolution fusion | flops 1019215872 | bytes 10764288 | tf_op jit(solution)/shard_map/dot_general | solution.py:535
Async XLA Ops:
  0.7 1.7 copy-start
  2.4 27.3 %copy-start.1 = (bf16[192,6912]{1,0:T(8,128)(2,1)S(1)}, bf16[192,6912]{1,0:T(8,128)(2,1)}, u32[]{:S(2)}) copy-start(bf16[192,6912]{1,0:T(8,128)(2,1)} %states.5) | copy-start | bytes 7962628
  8.5 21.2 %collective-permute-start = (bf16[1728,128]{1,0:T(8,128)(2,1)S(1)}, bf16[1728,128]{1,0:T(8,128)(2,1)S(1)}, u32[]{:S(2)}, u32[]{:S(2)}) collective-permute-start(bf16[1728,128]{1,0:T(8,128)(2,1)S(1)} %gather_faces.1), channel_id=1, source_target_pairs={{0,254},{2,0},{4,2},{6,4},{8,6},{10,8},{12,10},{14,12},{16,14},{18... | collective-permute-start | bytes 1327112 | tf_op jit(solution)/shard_map/ppermute | solution.py:31
  22.5 7.2 %copy-start.2 = (s32[8,4,384]{2,1,0:T(4,128)S(1)}, s32[8,4,384]{2,1,0:T(4,128)}, u32[]{:S(2)}) copy-start(s32[8,4,384]{2,1,0:T(4,128)} %reshape.7.index) | copy-start | bytes 147460
  23.5 0.8 copy-start.3
  59.2 25.8 %collective-permute-start.1 = (f32[1728,128]{1,0:T(8,128)S(1)}, f32[1728,128]{1,0:T(8,128)S(1)}, u32[]{:S(2)}, u32[]{:S(2)}) collective-permute-start(f32[1728,128]{1,0:T(8,128)S(1)} %get-tuple-element.13), channel_id=1, source_target_pairs={{0,2},{2,4},{4,6},{6,8},{8,10},{10,12},{12,14},{14,16},{16,18},{18... | collective-permute-start | bytes 2654216 | tf_op jit(solution)/shard_map/ppermute | solution.py:31
  59.2 25.7 %collective-permute-start.2 = (f32[1728,128]{1,0:T(8,128)S(1)}, f32[1728,128]{1,0:T(8,128)S(1)}, u32[]{:S(2)}, u32[]{:S(2)}) collective-permute-start(f32[1728,128]{1,0:T(8,128)S(1)} %get-tuple-element.14), channel_id=1, source_target_pairs={{0,254},{2,0},{4,2},{6,4},{8,6},{10,8},{12,10},{14,12},{16,14},{18... | collective-permute-start | bytes 2654216 | tf_op jit(solution)/shard_map/ppermute | solution.py:31
  112.0 25.1 %collective-permute-start.3 = (f32[1728,128]{1,0:T(8,128)S(1)}, f32[1728,128]{1,0:T(8,128)S(1)}, u32[]{:S(2)}, u32[]{:S(2)}) collective-permute-start(f32[1728,128]{1,0:T(8,128)S(1)} %get-tuple-element.16), channel_id=1, source_target_pairs={{0,2},{2,4},{4,6},{6,8},{8,10},{10,12},{12,14},{14,16},{16,18},{18... | collective-permute-start | bytes 2654216 | tf_op jit(solution)/shard_map/ppermute | solution.py:31

commit v6 on v5

--- a/solution.py
+++ b/solution.py
@@ -93,24 +93,17 @@
 
 
 def fill_table(width, states, table):
-    rows = lax.broadcasted_iota(jnp.int32, (LANES, LANES), 0)
-    columns = lax.broadcasted_iota(jnp.int32, (LANES, LANES), 1)
-    identity = jnp.where(rows == columns, 1.0, 0.0).astype(states.dtype)
-
     def one(tile, carry):
         nodes = pl.ds(pl.multiple_of(tile * LANES, LANES), LANES)
-        values = jnp.concatenate(
-            [states[:, nodes], jnp.zeros((2 * LANES - width, LANES), states.dtype)], axis=0
-        )
-        turned = lax.dot_general(
-            identity, values, (((1,), (1,)), ((), ())), preferred_element_type=jnp.float32
-        )
+        low = states[:LANES, nodes].astype(jnp.float32)
+        high = states[LANES:width, nodes].astype(jnp.float32)
+        high = jnp.concatenate([high, jnp.zeros((2 * LANES - width, LANES), jnp.float32)], axis=0)
         start = tile_start(tile)
-        table[even(start), :] = turned[:, :LANES]
-        table[even(start + 1), :] = turned[:, LANES:]
-        return carry
-
-    lax.fori_loop(0, states.shape[1] // LANES, one, 0, unroll=3)
+        table[even(start), :] = low.T
+        table[even(start + 1), :] = high.T
+        return carry
+
+    lax.fori_loop(0, states.shape[1] // LANES, one, 0, unroll=2)
 
 
 def spread_kernel(potential, factor):
@@ -121,7 +114,7 @@
         factor[even(start + 1), :] = value
         return carry
 
-    lax.fori_loop(0, potential.shape[0], one, 0)
+    lax.fori_loop(0, potential.shape[0], one, 0, unroll=2)
 
 
 def copy_rows(source, target, count):
@@ -334,16 +327,45 @@
 X_SIZE, Y_SIZE, Z_SIZE = 4, 4, 8
 PLANE = X_SIZE * Y_SIZE
 MESH = pl.DeviceIdType.MESH
-EXACT = lax.Precision.HIGHEST
-CHUNK = 768
 
 
 def across(left, right):
     return lax.dot_general(left, right, (((1,), (1,)), ((), ())), preferred_element_type=jnp.float32)
 
 
-def product_of(left, right):
-    return jnp.dot(left, right, precision=EXACT, preferred_element_type=jnp.float32)
+LEFT_PARTS = (2, 0, 1, 1, 0, 0)
+RIGHT_PARTS = (0, 2, 1, 0, 1, 0)
+
+
+def parts_of(value):
+    high = value.astype(jnp.bfloat16)
+    rest = value - high.astype(jnp.float32)
+    middle = rest.astype(jnp.bfloat16)
+    return high, middle, (rest - middle.astype(jnp.float32)).astype(jnp.bfloat16)
+
+
+def put_left(ref, value):
+    rows, size = value.shape
+    parts = parts_of(value)
+    for number, part in enumerate(LEFT_PARTS):
+        ref[:rows, number * size : (number + 1) * size] = parts[part]
+
+
+def put_right(ref, value):
+    size = value.shape[0]
+    parts = parts_of(value)
+    for number, part in enumerate(RIGHT_PARTS):
+        ref[number * size : (number + 1) * size, :] = parts[part]
+
+
+def product_of(left, right, rows):
+    return jnp.dot(left[:rows, :], right[...], preferred_element_type=jnp.float32)
+
+
+def three_less(offset, value):
+    row_ids = lax.broadcasted_iota(jnp.int32, value.shape, 0) + offset
+    column_ids = lax.broadcasted_iota(jnp.int32, value.shape, 1)
+    return jnp.where(row_ids == column_ids, 3.0, 0.0) - value
 
 
 def unpack(packed):
@@ -354,10 +376,18 @@
     return square, mixed
 
 
+def pack_share(ref, square, mixed, start, half):
+    some = mixed[pl.ds(start, half), :]
+    ref[:192, :] = square[:, :128]
+    ref[192:288, :] = some[:, :128]
+    ref[288:352, :] = jnp.concatenate([some[:64, 128:], square[128:, 128:]], axis=1)
+    ref[352:384, :] = jnp.concatenate([some[64:, 128:], jnp.zeros((32, 64), jnp.float32)], axis=1)
+
+
 def root_kernel(
     own, every, root_rows,
-    share, inbox, part, levels, own_all, other_all, square, mixed, current, inverse,
-    state_sems, here_sem, send_sems, plane_sems, level_sems, gather_sems, pair_sems,
+    share, inbox, part, levels, own_all, other_all, sent, received, own_sum, other_sum, mixed, current, inverse, factor, left, right,
+    state_sems, share_sems, here_sem, send_sems, plane_sems, level_sems, gather_sems, pair_sems,
 ):
     brick, side = lax.axis_index("brick"), lax.axis_index("state")
     width, owned = own.shape
@@ -381,46 +411,50 @@
     pl.semaphore_wait(barrier, PLANE + Z_SIZE - 1)
 
     pieces = 3
-    piece = owned // pieces
+    piece = owned // 2 // pieces
     place_here = pl.ds(pl.multiple_of(side * width, 16), width)
     here = pltpu.make_async_copy(own, every.at[place_here, :], here_sem)
     here.start()
-    states = []
-    for number in range(pieces):
-        columns = pl.ds(number * piece, piece)
+
+    def columns(part, number):
+        return pl.ds(pl.multiple_of(part * (owned // 2) + number * piece, 128), piece)
+
+    def swap_states(part, number, slot):
+        some = columns(part, number)
         copy = pltpu.make_async_remote_copy(
-            src_ref=own.at[:, columns], dst_ref=every.at[place_here, columns],
-            send_sem=state_sems.at[0, number], recv_sem=state_sems.at[1, number],
+            src_ref=own.at[:, some], dst_ref=every.at[place_here, some],
+            send_sem=state_sems.at[0, slot], recv_sem=state_sems.at[1, slot],
             device_id=(brick, 1 - side), device_id_type=MESH,
         )
         copy.start()
-        states.append(copy)
-
-    square[...] = jnp.zeros_like(square)
+        return copy
+
+    needed = [swap_states(1 - side, number, number) for number in range(pieces)]
+    own_sum[...] = jnp.zeros_like(own_sum)
+    for number in range(pieces):
+        values = own[:, columns(side, number)]
+        own_sum[...] += across(values, values)
+    here.wait()
+    other_sum[...] = jnp.zeros_like(other_sum)
     mixed[...] = jnp.zeros_like(mixed)
-
-    def add_square(number, carry):
-        values = own[:, pl.ds(pl.multiple_of(number * CHUNK, CHUNK), CHUNK)]
-        square[...] += across(values, values)
-        return carry
-
-    lax.fori_loop(0, owned // CHUNK, add_square, 0)
-    here.wait()
-    some = pl.ds(pl.multiple_of(side * half, 16), half)
-    for number, copy in enumerate(states):
+    place_there = pl.ds(pl.multiple_of((1 - side) * width, 16), width)
+    for number, copy in enumerate(needed):
         copy.wait()
-
-        def add_mixed(step, carry):
-            columns = pl.ds(pl.multiple_of(number * piece + step * CHUNK, CHUNK), CHUNK)
-            mixed[...] += across(every[some, columns], every[width:, columns])
-            return carry
-
-        lax.fori_loop(0, piece // CHUNK, add_mixed, 0)
-
-    share[:192, :] = square[:, :128]
-    share[192:288, :] = mixed[:, :128]
-    share[288:352, :] = jnp.concatenate([mixed[:64, 128:], square[128:, 128:]], axis=1)
-    share[352:384, :] = jnp.concatenate([mixed[64:, 128:], jnp.zeros((32, 64), jnp.float32)], axis=1)
+        some = columns(side, number)
+        values = every[place_there, some]
+        other_sum[...] += across(values, values)
+        mixed[...] += across(every[:width, some], every[width:, some])
+    rest = [swap_states(side, number, pieces + number) for number in range(pieces)]
+
+    pack_share(sent, other_sum, mixed, pl.multiple_of((1 - side) * half, 8), half)
+    swap = pltpu.make_async_remote_copy(
+        src_ref=sent, dst_ref=received, send_sem=share_sems.at[0], recv_sem=share_sems.at[1],
+        device_id=(brick, 1 - side), device_id_type=MESH,
+    )
+    swap.start()
+    pack_share(share, own_sum, mixed, pl.multiple_of(side * half, 8), half)
+    swap.wait()
+    share[...] += received[...]
 
     rows = share.shape[0] // PLANE
     copies = []
@@ -482,23 +516,29 @@
         [jnp.concatenate([first, both], axis=1), jnp.concatenate([both.T, second], axis=1)], axis=0
     )
     scale = jnp.sqrt(jnp.sum(margin * margin, axis=(0, 1), keepdims=True) + epsilon)
-    total = margin.shape[0]
-    row_ids = lax.broadcasted_iota(jnp.int32, (total, total), 0)
-    column_ids = lax.broadcasted_iota(jnp.int32, (total, total), 1)
-    three = jnp.where(row_ids == column_ids, 3.0, 0.0)
     start = margin / scale
-    factor = three - start
-    current[...] = 0.5 * product_of(factor, start)
-    inverse[...] = 0.5 * factor
+    value = three_less(0, start)
+    inverse[...] = 0.5 * value
+    put_left(left, value)
+    put_right(right, start)
+    current[...] = 0.5 * product_of(left, right, 2 * width)
+    put_right(right, current[...])
     for step in range(1, NS_STEPS - 1):
-        factor = three - product_of(inverse[...], current[...])
-        current[...] = 0.5 * product_of(factor, current[...])
-        inverse[...] = 0.5 * product_of(factor, inverse[...])
-    mine = pl.ds(pl.multiple_of(side * width, 8), width)
-    row_ids = lax.broadcasted_iota(jnp.int32, (width, total), 0) + side * width
-    column_ids = lax.broadcasted_iota(jnp.int32, (width, total), 1)
-    factor = jnp.where(row_ids == column_ids, 3.0, 0.0) - product_of(inverse[mine, :], current[...])
-    root_rows[...] = (0.5 * product_of(factor, inverse[...])).astype(root_rows.dtype)
+        put_left(left, inverse[...])
+        factor[...] = three_less(0, product_of(left, right, 2 * width))
+        put_left(left, factor[...])
+        current[...] = 0.5 * product_of(left, right, 2 * width)
+        put_right(right, inverse[...])
+        inverse[...] = 0.5 * product_of(left, right, 2 * width)
+        put_right(right, current[...])
+    first_row = pl.multiple_of(side * width, 16)
+    put_left(left, inverse[pl.ds(first_row, width), :])
+    factor[:width, :] = three_less(first_row, product_of(left, right, width))
+    put_left(left, factor[:width, :])
+    put_right(right, inverse[...])
+    root_rows[...] = (0.5 * product_of(left, right, width)).astype(root_rows.dtype)
+    for copy in rest:
+        copy.wait()
 
 
 def inverse_root(filtered):
@@ -518,9 +558,11 @@
         scratch_shapes=[
             VMEM((384, 128), f32), VMEM((PLANE - 1, rows, 128), f32), VMEM((rows, 128), f32),
             VMEM((Z_SIZE, rows, 128), f32), VMEM((PLANE, rows, 128), f32), VMEM((PLANE, rows, 128), f32),
-            VMEM((width, width), f32), VMEM((width // 2, width), f32),
-            VMEM((2 * width, 2 * width), f32), VMEM((2 * width, 2 * width), f32),
-            dma((2, 3)), dma, dma((2 * PLANE + Z_SIZE - 3,)), dma((PLANE - 1,)), dma((Z_SIZE - 1,)),
+            VMEM((384, 128), f32), VMEM((384, 128), f32),
+            VMEM((width, width), f32), VMEM((width, width), f32), VMEM((width, width), f32),
+            VMEM((2 * width, 2 * width), f32), VMEM((2 * width, 2 * width), f32), VMEM((2 * width, 2 * width), f32),
+            VMEM((2 * width, 12 * width), jnp.bfloat16), VMEM((12 * width, 2 * width), jnp.bfloat16),
+            dma((2, 6)), dma((2,)), dma, dma((2 * PLANE + Z_SIZE - 3,)), dma((PLANE - 1,)), dma((Z_SIZE - 1,)),
             dma((PLANE - 1,)), dma((2,)),
         ],
         compiler_params=pltpu.CompilerParams(

time: 185 us -> 182 us (0.984)
  Pallas kernels: 112 us -> 107 us
    pallas_call x1, Pallas kernels: 5.45 us -> 2.74 us  [filter_states(): pl.pallas_call(spread_kernel, name='spread_potential', out_shape=jax.Shap...]
  transfers between devices with their start and end apart: 4 -> 4, of which waited for: 2 -> 3; matrix products, arithmetic and copies ran while one was open for 2% -> 2% of each run, Pallas kernels for 3% -> 2%
where the time goes in v6:
time: 182 us
  Pallas kernels  107 us (59%)
  waiting for transfers between devices  44.3 us (24%)
  starting transfers between devices  19.4 us (11%)
  local copies, waits for them, and re-layouts  5.54 us (3%)
  matrix products  3.96 us (2%)
    ppermute x4, waiting for transfers between devices, passed_along(): return lax.ppermute(value, axis, pairs)  44.3 us
    pallas_call x1, Pallas kernels, inverse_root(): pl.pallas_call(root_kernel, name='inverse_root', out_shape=(jax.ShapeDtyp...  38.7 us
    pallas_call x1, Pallas kernels, filter_states(): pl.pallas_call(functools.partial(first_kernel, width, slots), name='first...  27.6 us
    pallas_call x1, Pallas kernels, filter_states(): pl.pallas_call(functools.partial(second_kernel, owned, slots), name='seco...  27.1 us
    ppermute x4, starting transfers between devices, passed_along(): return lax.ppermute(value, axis, pairs)  19.4 us
    pallas_call x1, Pallas kernels, filter_states(): pl.pallas_call(functools.partial(last_kernel, width), name='finish_filter...  6.26 us
    pallas_call x1, Pallas kernels, filter_states(): pl.pallas_call(functools.partial(faces_kernel, width), name='gather_faces...  4.38 us
    dot_general x1, matrix products, local(): return jnp.dot(root_rows, every, preferred_element_type=jnp.float32)  3.96 us
  transfers between devices with their start and end apart: 4, of which 3 were waited for; matrix products, arithmetic and copies ran while one was open for 2% of the time, Pallas kernels for 2%

profile of v6, /device:TPU:1, one launch (start us, length us, event | category | flops | bytes accessed | tf_op | source)
XLA Modules:
  0.0 181.5 jit_solution(242982965444621899)
XLA Ops:
  0.0 0.7 broadcast_multiply_fusion.1.face
  0.7 0.0 copy-start
  0.7 1.7 copy-done
  2.4 0.0 copy-start.1
  2.5 4.4 %gather_faces.1 = bf16[1728,128]{1,0:T(8,128)(2,1)S(1)} custom-call(bf16[192,6912]{1,0:T(8,128)(2,1)S(1)} %copy-done, s32[1152]{0:T(1024)S(1)} %broadcast_multiply_fusion.1.face), custom_call_target="tpu_custom_call" | custom-call | tf_op jit(solution)/shard_map/gather_faces/pallas_call | solution.py:285
  6.8 11.1 %collective-permute-start = (bf16[1728,128]{1,0:T(8,128)(2,1)S(1)}, bf16[1728,128]{1,0:T(8,128)(2,1)S(1)}, u32[]{:S(2)}, u32[]{:S(2)}) collective-permute-start(bf16[1728,128]{1,0:T(8,128)(2,1)S(1)} %gather_faces.1), channel_id=1, source_target_pairs={{0,254},{2,0},{4,2},{6,4},{8,6},{10,8},{12,10},{14,12},{16,14},{18... | collective-permute-start | bytes 1327112 | tf_op jit(solution)/shard_map/ppermute | solution.py:31
  17.9 0.8 broadcast_multiply_fusion
  18.7 0.6 pad.9
  19.4 1.4 reshape.7.index
  20.8 0.0 copy-start.2
  20.8 1.0 pad.8.kinetic
  21.8 0.0 copy-start.3
  21.8 0.7 copy-done.3
  22.5 2.7 %spread_potential.1.potential = f32[13824,128]{1,0:T(8,128)S(1)} custom-call(f32[54,128]{1,0:T(8,128)S(1)} %bitcast.3), custom_call_target="tpu_custom_call" | custom-call | flops 1769472 | bytes 21233664 | tf_op jit(solution)/shard_map/spread_potential/pallas_call | solution.py:264
  25.3 1.5 collective-permute-done.ghosts
  26.8 0.0 copy-done.1
  26.8 0.0 copy-done.2
  26.8 27.6 %first_apply.1 = (f32[16128,128]{1,0:T(8,128)S(1)}, f32[1728,128]{1,0:T(8,128)S(1)}, f32[1728,128]{1,0:T(8,128)S(1)}) custom-call(bf16[192,6912]{1,0:T(8,128)(2,1)S(1)} %copy-done.1, bf16[1728,128]{1,0:T(8,128)(2,1)S(1)} %collective-permute-done.ghosts, f32[13824,128]{1,0:T(8,128)S(1)} %spread_potential.1.potential, bf16[352,352]{1,0:T(8,128)(2,1)S(1)} %pad.8.kinetic, ...), custom_call_target="tpu_custom_call" | custom-call | tf_op jit(solution)/shard_map/first_apply/pallas_call | solution.py:295
  54.4 0.1 collective-permute-start.1
  54.5 7.9 %collective-permute-start.2 = (f32[1728,128]{1,0:T(8,128)S(1)}, f32[1728,128]{1,0:T(8,128)S(1)}, u32[]{:S(2)}, u32[]{:S(2)}) collective-permute-start(f32[1728,128]{1,0:T(8,128)S(1)} %get-tuple-element.14), channel_id=1, source_target_pairs={{0,254},{2,0},{4,2},{6,4},{8,6},{10,8},{12,10},{14,12},{16,14},{18... | collective-permute-start | bytes 2654216 | tf_op jit(solution)/shard_map/ppermute | solution.py:31
  62.4 18.2 %collective-permute-done.1.returned = f32[1728,128]{1,0:T(8,128)S(1)} collective-permute-done((f32[1728,128]{1,0:T(8,128)S(1)}, f32[1728,128]{1,0:T(8,128)S(1)}, u32[]{:S(2)}, u32[]{:S(2)}) %collective-permute-start.1) | collective-permute-done | bytes 884768 | tf_op jit(solution)/shard_map/ppermute | solution.py:31
  80.7 0.0 collective-permute-done.2.ghost_sums
  80.7 27.1 %second_apply.1 = (f32[13824,128]{1,0:T(8,128)S(1)}, f32[1728,128]{1,0:T(8,128)S(1)}) custom-call(f32[16128,128]{1,0:T(8,128)S(1)} %get-tuple-element.12.given, f32[1728,128]{1,0:T(8,128)S(1)} %collective-permute-done.1.returned, f32[1728,128]{1,0:T(8,128)S(1)} %collective-permute-done.2.ghost_sums, f32[13824,128]{1,0:T(8,128)S(1)} %spread_potential.1.potential, ...), custom_call_target="tpu_custom_call" | custom-call | tf_op jit(solution)/shard_map/second_apply/pallas_call | solution.py:306
  107.7 0.3 collective-permute-start.3
  108.0 24.5 %collective-permute-done.3.returned = f32[1728,128]{1,0:T(8,128)S(1)} collective-permute-done((f32[1728,128]{1,0:T(8,128)S(1)}, f32[1728,128]{1,0:T(8,128)S(1)}, u32[]{:S(2)}, u32[]{:S(2)}) %collective-permute-start.3) | collective-permute-done | bytes 884768 | tf_op jit(solution)/shard_map/ppermute | solution.py:31
  132.6 6.3 %finish_filter.1.own = bf16[192,6912]{1,0:T(8,128)(2,1)S(1)} custom-call(f32[13824,128]{1,0:T(8,128)S(1)} %get-tuple-element.15.given, bf16[192,6912]{1,0:T(8,128)(2,1)S(1)} %copy-done.1, f32[1728,128]{1,0:T(8,128)S(1)} %collective-permute-done.3.returned, s32[1152]{0:T(1024)S(1)} %broadcast_multiply_fusion.1.face), custom_call_target="tpu_custom_call" | custom-call | tf_op jit(solution)/shard_map/finish_filter/pallas_call | solution.py:316
  138.8 38.7 %inverse_root.1 = (bf16[384,6912]{1,0:T(8,128)(2,1)S(1)}, bf16[192,384]{1,0:T(8,128)(2,1)S(1)}) custom-call(bf16[192,6912]{1,0:T(8,128)(2,1)S(1)} %finish_filter.1.own), custom_call_target="tpu_custom_call" | custom-call | tf_op jit(solution)/shard_map/inverse_root/pallas_call | solution.py:549
  177.6 4.0 %fusion = f32[192,6912]{1,0:T(8,128)} fusion(bf16[192,384]{1,0:T(8,128)(2,1)S(1)} %get-tuple-element.17, bf16[384,6912]{1,0:T(8,128)(2,1)S(1)} %get-tuple-element.18), kind=kOutput, calls=%fused_computation.2 | convolution fusion | flops 1019215872 | bytes 10764288 | tf_op jit(solution)/shard_map/dot_general | solution.py:577
Async XLA Ops:
  0.7 1.7 copy-start
  2.4 24.3 %copy-start.1 = (bf16[192,6912]{1,0:T(8,128)(2,1)S(1)}, bf16[192,6912]{1,0:T(8,128)(2,1)}, u32[]{:S(2)}) copy-start(bf16[192,6912]{1,0:T(8,128)(2,1)} %states.5) | copy-start | bytes 7962628
  6.8 20.0 %collective-permute-start = (bf16[1728,128]{1,0:T(8,128)(2,1)S(1)}, bf16[1728,128]{1,0:T(8,128)(2,1)S(1)}, u32[]{:S(2)}, u32[]{:S(2)}) collective-permute-start(bf16[1728,128]{1,0:T(8,128)(2,1)S(1)} %gather_faces.1), channel_id=1, source_target_pairs={{0,254},{2,0},{4,2},{6,4},{8,6},{10,8},{12,10},{14,12},{16,14},{18... | collective-permute-start | bytes 1327112 | tf_op jit(solution)/shard_map/ppermute | solution.py:31
  20.8 6.0 %copy-start.2 = (s32[8,4,384]{2,1,0:T(4,128)S(1)}, s32[8,4,384]{2,1,0:T(4,128)}, u32[]{:S(2)}) copy-start(s32[8,4,384]{2,1,0:T(4,128)} %reshape.7.index) | copy-start | bytes 147460
  21.8 0.8 copy-start.3
  54.4 26.2 %collective-permute-start.1 = (f32[1728,128]{1,0:T(8,128)S(1)}, f32[1728,128]{1,0:T(8,128)S(1)}, u32[]{:S(2)}, u32[]{:S(2)}) collective-permute-start(f32[1728,128]{1,0:T(8,128)S(1)} %get-tuple-element.13), channel_id=1, source_target_pairs={{0,2},{2,4},{4,6},{6,8},{8,10},{10,12},{12,14},{14,16},{16,18},{18... | collective-permute-start | bytes 2654216 | tf_op jit(solution)/shard_map/ppermute | solution.py:31
  54.5 26.1 %collective-permute-start.2 = (f32[1728,128]{1,0:T(8,128)S(1)}, f32[1728,128]{1,0:T(8,128)S(1)}, u32[]{:S(2)}, u32[]{:S(2)}) collective-permute-start(f32[1728,128]{1,0:T(8,128)S(1)} %get-tuple-element.14), channel_id=1, source_target_pairs={{0,254},{2,0},{4,2},{6,4},{8,6},{10,8},{12,10},{14,12},{16,14},{18... | collective-permute-start | bytes 2654216 | tf_op jit(solution)/shard_map/ppermute | solution.py:31
  107.7 24.8 %collective-permute-start.3 = (f32[1728,128]{1,0:T(8,128)S(1)}, f32[1728,128]{1,0:T(8,128)S(1)}, u32[]{:S(2)}, u32[]{:S(2)}) collective-permute-start(f32[1728,128]{1,0:T(8,128)S(1)} %get-tuple-element.16), channel_id=1, source_target_pairs={{0,2},{2,4},{4,6},{6,8},{8,10},{10,12},{12,14},{14,16},{16,18},{18... | collective-permute-start | bytes 2654216 | tf_op jit(solution)/shard_map/ppermute | solution.py:31

commit v7 on v5

--- a/solution.py
+++ b/solution.py
@@ -93,24 +93,17 @@
 
 
 def fill_table(width, states, table):
-    rows = lax.broadcasted_iota(jnp.int32, (LANES, LANES), 0)
-    columns = lax.broadcasted_iota(jnp.int32, (LANES, LANES), 1)
-    identity = jnp.where(rows == columns, 1.0, 0.0).astype(states.dtype)
-
     def one(tile, carry):
         nodes = pl.ds(pl.multiple_of(tile * LANES, LANES), LANES)
-        values = jnp.concatenate(
-            [states[:, nodes], jnp.zeros((2 * LANES - width, LANES), states.dtype)], axis=0
-        )
-        turned = lax.dot_general(
-            identity, values, (((1,), (1,)), ((), ())), preferred_element_type=jnp.float32
-        )
+        low = states[:LANES, nodes].astype(jnp.float32)
+        high = states[LANES:width, nodes].astype(jnp.float32)
+        high = jnp.concatenate([high, jnp.zeros((2 * LANES - width, LANES), jnp.float32)], axis=0)
         start = tile_start(tile)
-        table[even(start), :] = turned[:, :LANES]
-        table[even(start + 1), :] = turned[:, LANES:]
-        return carry
-
-    lax.fori_loop(0, states.shape[1] // LANES, one, 0, unroll=3)
+        table[even(start), :] = low.T
+        table[even(start + 1), :] = high.T
+        return carry
+
+    lax.fori_loop(0, states.shape[1] // LANES, one, 0, unroll=2)
 
 
 def spread_kernel(potential, factor):
@@ -121,7 +114,7 @@
         factor[even(start + 1), :] = value
         return carry
 
-    lax.fori_loop(0, potential.shape[0], one, 0)
+    lax.fori_loop(0, potential.shape[0], one, 0, unroll=2)
 
 
 def copy_rows(source, target, count):
@@ -218,22 +211,21 @@
 
 
 def second_kernel(
-    owned, slots, given, returned, ghost_sums, potential, kinetic, index, face, sums, ghost_out,
+    owned, slots, given, returned, ghost_sums, potential, kinetic, index, face, summed, sums, ghost_out,
     table, total, held, product, places, sems,
 ):
     face_count = face.shape[0]
     rows_all = table.shape[0]
-    copy_rows(given, table, rows_all)
-    add_returned(table, returned, face, held)
+    add_returned(summed, returned, face, held)
     for tile in range(face_count // LANES):
         start = 2 * owned + tile * 2 * LANES
         low, high = unpack_rows(ghost_sums, tile)
-        table[even(start), :] = table[even(start), :] + low
-        table[even(start + 1), :] = table[even(start + 1), :] + high
+        summed[even(start), :] = summed[even(start), :] + low
+        summed[even(start + 1), :] = summed[even(start + 1), :] + high
 
     def scale(tile, carry):
         rows = pl.ds(tile_start(tile), 2 * LANES)
-        table[rows, :] = (table[rows, :] / cheb_half).astype(jnp.bfloat16).astype(jnp.float32)
+        table[rows, :] = (summed[rows, :] / cheb_half).astype(jnp.bfloat16).astype(jnp.float32)
         return carry
 
     lax.fori_loop(0, rows_all // (2 * LANES), scale, 0)
@@ -245,7 +237,6 @@
 
 def last_kernel(width, given, states, returned, face, filtered, total, held):
     owned = filtered.shape[1]
-    copy_rows(given, total, 2 * owned)
     add_returned(total, returned, face, held)
 
     def one(tile, carry):
@@ -310,12 +301,13 @@
     )(states, ghosts, potential, kinetic, index, face)
     returned = passed_along(ghost_part, "brick", 1)
     ghost_sums = passed_along(face_part, "brick", -1)
-    second, ghost_part = pl.pallas_call(
+    _, second, ghost_part = pl.pallas_call(
         functools.partial(second_kernel, owned, slots),
         name="second_apply",
-        out_shape=(jax.ShapeDtypeStruct((2 * owned, LANES), f32), sums),
+        out_shape=(field, jax.ShapeDtypeStruct((2 * owned, LANES), f32), sums),
         in_specs=[block(VMEM)] * 5 + [block(pl.ANY), block(SMEM)],
-        out_specs=(block(VMEM),) * 2,
+        out_specs=(block(VMEM),) * 3,
+        input_output_aliases={0: 0},
         scratch_shapes=[table, table] + work,
         compiler_params=params,
     )(first, returned, ghost_sums, potential, kinetic, index, face)
@@ -323,12 +315,16 @@
     return pl.pallas_call(
         functools.partial(last_kernel, width),
         name="finish_filter",
-        out_shape=jax.ShapeDtypeStruct((width, owned), jnp.bfloat16),
+        out_shape=(
+            jax.ShapeDtypeStruct((width, owned), jnp.bfloat16),
+            jax.ShapeDtypeStruct((2 * owned, LANES), f32),
+        ),
         in_specs=[block(VMEM)] * 3 + [block(SMEM)],
-        out_specs=block(VMEM),
-        scratch_shapes=[VMEM((2 * owned, LANES), f32), faces_held],
+        out_specs=(block(VMEM),) * 2,
+        input_output_aliases={0: 1},
+        scratch_shapes=[faces_held],
         compiler_params=params,
-    )(second, states, returned, face)
+    )(second, states, returned, face)[0]
 
 
 X_SIZE, Y_SIZE, Z_SIZE = 4, 4, 8

time: 185 us -> 180 us (0.973)
  Pallas kernels: 112 us -> 105 us
    pallas_call x1, Pallas kernels: 5.45 us -> 2.74 us  [filter_states(): pl.pallas_call(spread_kernel, name='spread_potential', out_shape=jax.Shap...]
  transfers between devices with their start and end apart: 4 -> 4, of which waited for: 2 -> 3; matrix products, arithmetic and copies ran while one was open for 2% -> 2% of each run, Pallas kernels for 3% -> 2%
where the time goes in v7:
time: 180 us
  Pallas kernels  105 us (58%)
  waiting for transfers between devices  44.3 us (25%)
  starting transfers between devices  19.4 us (11%)
  local copies, waits for them, and re-layouts  5.54 us (3%)
  matrix products  3.93 us (2%)
    ppermute x4, waiting for transfers between devices, passed_along(): return lax.ppermute(value, axis, pairs)  44.3 us
    pallas_call x1, Pallas kernels, inverse_root(): pl.pallas_call(root_kernel, name='inverse_root', out_shape=(jax.ShapeDtyp...  37.8 us
    pallas_call x1, Pallas kernels, filter_states(): pl.pallas_call(functools.partial(first_kernel, width, slots), name='first...  27.7 us
    pallas_call x1, Pallas kernels, filter_states(): pl.pallas_call(functools.partial(second_kernel, owned, slots), name='seco...  26.7 us
    ppermute x4, starting transfers between devices, passed_along(): return lax.ppermute(value, axis, pairs)  19.4 us
    pallas_call x1, Pallas kernels, filter_states(): pl.pallas_call(functools.partial(last_kernel, width), name='finish_filter...  5.78 us
    pallas_call x1, Pallas kernels, filter_states(): pl.pallas_call(functools.partial(faces_kernel, width), name='gather_faces...  4.34 us
    dot_general x1, matrix products, local(): return jnp.dot(root_rows, every, preferred_element_type=jnp.float32)  3.93 us
  transfers between devices with their start and end apart: 4, of which 3 were waited for; matrix products, arithmetic and copies ran while one was open for 2% of the time, Pallas kernels for 2%

profile of v7, /device:TPU:1, one launch (start us, length us, event | category | flops | bytes accessed | tf_op | source)
XLA Modules:
  0.0 179.8 jit_solution(7919445831717482050)
XLA Ops:
  0.0 0.7 broadcast_multiply_fusion.1.face
  0.7 0.0 copy-start
  0.7 1.7 copy-done
  2.4 0.0 copy-start.1
  2.5 4.3 %gather_faces.1 = bf16[1728,128]{1,0:T(8,128)(2,1)S(1)} custom-call(bf16[192,6912]{1,0:T(8,128)(2,1)S(1)} %copy-done, s32[1152]{0:T(1024)S(1)} %broadcast_multiply_fusion.1.face), custom_call_target="tpu_custom_call" | custom-call | tf_op jit(solution)/shard_map/gather_faces/pallas_call | solution.py:283
  6.8 11.1 %collective-permute-start = (bf16[1728,128]{1,0:T(8,128)(2,1)S(1)}, bf16[1728,128]{1,0:T(8,128)(2,1)S(1)}, u32[]{:S(2)}, u32[]{:S(2)}) collective-permute-start(bf16[1728,128]{1,0:T(8,128)(2,1)S(1)} %gather_faces.1), channel_id=1, source_target_pairs={{0,254},{2,0},{4,2},{6,4},{8,6},{10,8},{12,10},{14,12},{16,14},{18... | collective-permute-start | bytes 1327112 | tf_op jit(solution)/shard_map/ppermute | solution.py:31
  17.9 0.8 broadcast_multiply_fusion
  18.7 0.6 pad.9
  19.3 1.4 reshape.7.index
  20.8 0.0 copy-start.2
  20.8 1.0 pad.8.kinetic
  21.8 0.0 copy-start.3
  21.8 0.7 copy-done.3
  22.5 2.7 %spread_potential.1.potential = f32[13824,128]{1,0:T(8,128)S(1)} custom-call(f32[54,128]{1,0:T(8,128)S(1)} %bitcast.3), custom_call_target="tpu_custom_call" | custom-call | flops 1769472 | bytes 21233664 | tf_op jit(solution)/shard_map/spread_potential/pallas_call | solution.py:262
  25.3 1.5 collective-permute-done.ghosts
  26.8 0.0 copy-done.1
  26.8 0.0 copy-done.2
  26.8 27.7 %first_apply.1 = (f32[16128,128]{1,0:T(8,128)S(1)}, f32[1728,128]{1,0:T(8,128)S(1)}, f32[1728,128]{1,0:T(8,128)S(1)}) custom-call(bf16[192,6912]{1,0:T(8,128)(2,1)S(1)} %copy-done.1, bf16[1728,128]{1,0:T(8,128)(2,1)S(1)} %collective-permute-done.ghosts, f32[13824,128]{1,0:T(8,128)S(1)} %spread_potential.1.potential, bf16[352,352]{1,0:T(8,128)(2,1)S(1)} %pad.8.kinetic, ...), custom_call_target="tpu_custom_call" | custom-call | tf_op jit(solution)/shard_map/first_apply/pallas_call | solution.py:293
  54.5 0.1 collective-permute-start.1
  54.6 7.9 %collective-permute-start.2 = (f32[1728,128]{1,0:T(8,128)S(1)}, f32[1728,128]{1,0:T(8,128)S(1)}, u32[]{:S(2)}, u32[]{:S(2)}) collective-permute-start(f32[1728,128]{1,0:T(8,128)S(1)} %get-tuple-element.15), channel_id=1, source_target_pairs={{0,254},{2,0},{4,2},{6,4},{8,6},{10,8},{12,10},{14,12},{16,14},{18... | collective-permute-start | bytes 2654216 | tf_op jit(solution)/shard_map/ppermute | solution.py:31
  62.5 18.2 %collective-permute-done.1.returned = f32[1728,128]{1,0:T(8,128)S(1)} collective-permute-done((f32[1728,128]{1,0:T(8,128)S(1)}, f32[1728,128]{1,0:T(8,128)S(1)}, u32[]{:S(2)}, u32[]{:S(2)}) %collective-permute-start.1) | collective-permute-done | bytes 884768 | tf_op jit(solution)/shard_map/ppermute | solution.py:31
  80.7 0.0 collective-permute-done.2.ghost_sums
  80.7 26.7 %second_apply.1 = (f32[16128,128]{1,0:T(8,128)S(1)}, f32[13824,128]{1,0:T(8,128)S(1)}, f32[1728,128]{1,0:T(8,128)S(1)}) custom-call(f32[16128,128]{1,0:T(8,128)S(1)} %get-tuple-element.13.given, f32[1728,128]{1,0:T(8,128)S(1)} %collective-permute-done.1.returned, f32[1728,128]{1,0:T(8,128)S(1)} %collective-permute-done.2.ghost_sums, ...), custom_call_target="tpu_custom_call", output_to_operand_aliasing={{0}: (0, {})} | custom-call | tf_op jit(solution)/shard_map/second_apply/pallas_call | solution.py:304
  107.4 0.3 collective-permute-start.3
  107.7 24.5 %collective-permute-done.3.returned = f32[1728,128]{1,0:T(8,128)S(1)} collective-permute-done((f32[1728,128]{1,0:T(8,128)S(1)}, f32[1728,128]{1,0:T(8,128)S(1)}, u32[]{:S(2)}, u32[]{:S(2)}) %collective-permute-start.3) | collective-permute-done | bytes 884768 | tf_op jit(solution)/shard_map/ppermute | solution.py:31
  132.2 5.8 %finish_filter.1 = (bf16[192,6912]{1,0:T(8,128)(2,1)S(1)}, f32[13824,128]{1,0:T(8,128)S(1)}) custom-call(f32[13824,128]{1,0:T(8,128)S(1)} %get-tuple-element.16.given, bf16[192,6912]{1,0:T(8,128)(2,1)S(1)} %copy-done.1, f32[1728,128]{1,0:T(8,128)S(1)} %collective-permute-done.3.returned, ...), custom_call_target="tpu_custom_call", output_to_operand_aliasing={{1}: (0, {})} | custom-call | tf_op jit(solution)/shard_map/finish_filter/pallas_call | solution.py:315
  138.0 37.8 %inverse_root.1 = (bf16[384,6912]{1,0:T(8,128)(2,1)S(1)}, bf16[192,384]{1,0:T(8,128)(2,1)S(1)}) custom-call(bf16[192,6912]{1,0:T(8,128)(2,1)S(1)} %get-tuple-element.18.own), custom_call_target="tpu_custom_call" | custom-call | tf_op jit(solution)/shard_map/inverse_root/pallas_call | solution.py:505
  175.9 3.9 %fusion = f32[192,6912]{1,0:T(8,128)} fusion(bf16[192,384]{1,0:T(8,128)(2,1)S(1)} %get-tuple-element.19, bf16[384,6912]{1,0:T(8,128)(2,1)S(1)} %get-tuple-element.20), kind=kOutput, calls=%fused_computation.2 | convolution fusion | flops 1019215872 | bytes 10764288 | tf_op jit(solution)/shard_map/dot_general | solution.py:531
Async XLA Ops:
  0.7 1.7 copy-start
  2.4 24.3 %copy-start.1 = (bf16[192,6912]{1,0:T(8,128)(2,1)S(1)}, bf16[192,6912]{1,0:T(8,128)(2,1)}, u32[]{:S(2)}) copy-start(bf16[192,6912]{1,0:T(8,128)(2,1)} %states.5) | copy-start | bytes 7962628
  6.8 20.0 %collective-permute-start = (bf16[1728,128]{1,0:T(8,128)(2,1)S(1)}, bf16[1728,128]{1,0:T(8,128)(2,1)S(1)}, u32[]{:S(2)}, u32[]{:S(2)}) collective-permute-start(bf16[1728,128]{1,0:T(8,128)(2,1)S(1)} %gather_faces.1), channel_id=1, source_target_pairs={{0,254},{2,0},{4,2},{6,4},{8,6},{10,8},{12,10},{14,12},{16,14},{18... | collective-permute-start | bytes 1327112 | tf_op jit(solution)/shard_map/ppermute | solution.py:31
  20.8 6.0 %copy-start.2 = (s32[8,4,384]{2,1,0:T(4,128)S(1)}, s32[8,4,384]{2,1,0:T(4,128)}, u32[]{:S(2)}) copy-start(s32[8,4,384]{2,1,0:T(4,128)} %reshape.7.index) | copy-start | bytes 147460
  21.8 0.8 copy-start.3
  54.5 26.2 %collective-permute-start.1 = (f32[1728,128]{1,0:T(8,128)S(1)}, f32[1728,128]{1,0:T(8,128)S(1)}, u32[]{:S(2)}, u32[]{:S(2)}) collective-permute-start(f32[1728,128]{1,0:T(8,128)S(1)} %get-tuple-element.14), channel_id=1, source_target_pairs={{0,2},{2,4},{4,6},{6,8},{8,10},{10,12},{12,14},{14,16},{16,18},{18... | collective-permute-start | bytes 2654216 | tf_op jit(solution)/shard_map/ppermute | solution.py:31
  54.6 26.1 %collective-permute-start.2 = (f32[1728,128]{1,0:T(8,128)S(1)}, f32[1728,128]{1,0:T(8,128)S(1)}, u32[]{:S(2)}, u32[]{:S(2)}) collective-permute-start(f32[1728,128]{1,0:T(8,128)S(1)} %get-tuple-element.15), channel_id=1, source_target_pairs={{0,254},{2,0},{4,2},{6,4},{8,6},{10,8},{12,10},{14,12},{16,14},{18... | collective-permute-start | bytes 2654216 | tf_op jit(solution)/shard_map/ppermute | solution.py:31
  107.4 24.8 %collective-permute-start.3 = (f32[1728,128]{1,0:T(8,128)S(1)}, f32[1728,128]{1,0:T(8,128)S(1)}, u32[]{:S(2)}, u32[]{:S(2)}) collective-permute-start(f32[1728,128]{1,0:T(8,128)S(1)} %get-tuple-element.17), channel_id=1, source_target_pairs={{0,2},{2,4},{4,6},{6,8},{8,10},{10,12},{12,14},{14,16},{16,18},{18... | collective-permute-start | bytes 2654216 | tf_op jit(solution)/shard_map/ppermute | solution.py:31
